TPU v7x, 32 devices: a whole 2x2x4 slice. The times are simulated.
32 devices in a mesh: stream: 8 (over z, x), cross: 4 (over y, core).
Axes of the slice: x: 2, y: 2, z: 4, core: 2. Of those that a mesh axis runs over, the one named last changes fastest.
Arguments:
- adjoint: float32 [5, 32, 4096], P(None, 'stream', 'cross'), may hold values from -6 to 6
- source: float32 [5, 32, 4096], P(None, 'stream', 'cross'), may hold values from -30 to 30
- shape_grad: float32 [5, 32, 4096], P(None, 'stream', 'cross'), may hold values from -6 to 6
- lower_band: float32 [2, 5, 32, 4096], P(None, None, 'stream', 'cross'), may hold values from -1.5 to 0.5
- upper_band: float32 [3, 5, 32, 4096], P(None, None, 'stream', 'cross'), may hold values from -6 to 2, as said below
- jacobian: float32 [5, 5], replicated, may hold values from -2.5 to 2.5
- left_vectors: float32 [5, 5], replicated, may hold values from -1 to 2
- right_vectors: float32 [5, 5], replicated, may hold values from -1 to 2
- ctrl_local: int32 [32, 4096], P('stream', 'cross'), may hold values from 0 to 65535
Outputs:
- adjoint_next: float32 [5, 32, 4096], P(None, 'stream', 'cross')
- sensitivity: float32 [524288], P(('stream', 'cross'))
Inputs may be any that keep to these rules, and one draw needn't show every extreme that they name: upper_band[0] lies in 0.5 to 2.
All inputs are finite; a program needn't handle non-finite values.
Results may differ from a plain program's by a relative error of at most 0.00029.
Values sent between devices are 32-bit elements; how exact they have to be, the bound alone decides.
No kernel may reach another device: no remote copies, remote signals or barrier semaphores. Data moves between devices by JAX's collectives and lax.ppermute only.
A program may use at most 64 MiB of HBM per device.

v0:
```python
import jax
import jax.numpy as jnp
from jax import lax
from jax.sharding import PartitionSpec as P

NF = 5
NCTRL = 524288


dissipation = 0.25
step_scale = 0.5
epsilon = 1e-06


def with_halo(array, sides, width):
    for axis, dim in sides:
        size, length = (lax.axis_size(axis), array.shape[dim])
        up = [(i, (i + 1) % size) for i in range(size - 1)]
        down = [(j, i) for i, j in up]
        last = lax.slice_in_dim(array, length - width, length, axis=dim)
        first = lax.slice_in_dim(array, 0, width, axis=dim)
        before = lax.ppermute(last, axis, up)
        after = lax.ppermute(first, axis, down)
        array = jnp.concatenate([before, array, after], axis=dim)
    return array


def compose(earlier, later):
    return (
        later[0] * earlier[0] + later[1] * earlier[2],
        later[0] * earlier[1] + later[1] * earlier[3],
        later[2] * earlier[0] + later[3] * earlier[2],
        later[2] * earlier[1] + later[3] * earlier[3],
        later[0] * earlier[4] + later[1] * earlier[5] + later[4],
        later[2] * earlier[4] + later[3] * earlier[5] + later[5],
    )


def forward_maps(rhs_cells, first_sub, second_sub):
    unit_fill = jnp.ones_like(rhs_cells)
    zero_fill = jnp.zeros_like(rhs_cells)
    return (-first_sub, -second_sub, unit_fill, zero_fill, rhs_cells, zero_fill)


def backward_maps(rhs_cells, diag_cells, first_sup, second_sup):
    unit_fill = jnp.ones_like(rhs_cells)
    zero_fill = jnp.zeros_like(rhs_cells)
    return (
        -first_sup / diag_cells,
        -second_sup / diag_cells,
        unit_fill,
        zero_fill,
        rhs_cells / diag_cells,
        zero_fill,
    )


def line_scan(cell_maps, flipped):
    if flipped:
        cell_maps = tuple((jnp.flip(entry, 1) for entry in cell_maps))
    running = lax.associative_scan(compose, cell_maps, axis=1)
    if flipped:
        running = tuple((jnp.flip(entry, 1) for entry in running))
    return running


def solve_whole(pieces):
    rhs_cells, first_sub, second_sub, diag_cells, first_sup, second_sup = pieces
    forward = line_scan(forward_maps(rhs_cells, first_sub, second_sub), False)[4]
    return line_scan(backward_maps(forward, diag_cells, first_sup, second_sup), True)[4]


def shards(
    adjoint,
    source,
    shape_grad,
    lower_band,
    upper_band,
    jacobian,
    left_vectors,
    right_vectors,
    ctrl_local,
):
    highest = lax.Precision.HIGHEST
    contribution = jnp.sum(adjoint * shape_grad, axis=0)
    slab_size = NCTRL // lax.axis_size("stream")
    local_sums = jax.ops.segment_sum(
        contribution.ravel(), ctrl_local.ravel(), num_segments=slab_size
    )
    sensitivity = lax.psum_scatter(local_sums, "cross", scatter_dimension=0, tiled=True)
    padded = with_halo(adjoint, (("stream", 1),), 1)
    ahead_cells = padded[:, 2:, :]
    behind = padded[:, :-2, :]
    central = jnp.einsum("fg,gij->fij", jacobian, ahead_cells - behind, precision=highest)
    residual = source - 0.5 * central + dissipation * (ahead_cells - 2.0 * adjoint + behind)
    characteristic = jnp.einsum("fg,gij->fij", left_vectors, residual, precision=highest)
    packed = (
        characteristic,
        lower_band[0],
        lower_band[1],
        upper_band[0],
        upper_band[1],
        upper_band[2],
    )
    whole_lines = solve_whole(
        (
            lax.all_to_all(packed[0], "stream", split_axis=2, concat_axis=1, tiled=True),
            lax.all_to_all(packed[1], "stream", split_axis=2, concat_axis=1, tiled=True),
            lax.all_to_all(packed[2], "stream", split_axis=2, concat_axis=1, tiled=True),
            lax.all_to_all(packed[3], "stream", split_axis=2, concat_axis=1, tiled=True),
            lax.all_to_all(packed[4], "stream", split_axis=2, concat_axis=1, tiled=True),
            lax.all_to_all(packed[5], "stream", split_axis=2, concat_axis=1, tiled=True),
        )
    )
    solved = lax.all_to_all(whole_lines, "stream", split_axis=1, concat_axis=2, tiled=True)
    increment = jnp.einsum("fg,gij->fij", right_vectors, solved, precision=highest)
    squares = lax.psum(jnp.sum(increment * increment), ("stream", "cross"))
    cell_count = (
        NF * adjoint.shape[1] * adjoint.shape[2] * lax.axis_size("stream") * lax.axis_size("cross")
    )
    root_mean = jnp.sqrt(squares / cell_count + epsilon)
    adjoint_next = adjoint + step_scale * increment / root_mean
    return (adjoint_next, sensitivity)


def solution(mesh):
    in_specs = (
        P(None, "stream", "cross"),
        P(None, "stream", "cross"),
        P(None, "stream", "cross"),
        P(None, None, "stream", "cross"),
        P(None, None, "stream", "cross"),
        P(),
        P(),
        P(),
        P("stream", "cross"),
    )
    out_specs = (P(None, "stream", "cross"), P(("stream", "cross")))
    return jax.shard_map(shards, mesh=mesh, in_specs=in_specs, out_specs=out_specs, check_vma=False)
```

profile of v0, /device:TPU:0, one launch (start us, length us, event | category | flops | bytes accessed | tf_op | source)
XLA Modules:
  0.0 260.7 jit_solution(15421236842699910726)
XLA Ops:
  7.2 0.9 copy.81
  8.1 1.3 collective-permute-start
  9.4 5.5 %collective-permute-start.1 = (f32[5,1,1024]{2,0,1:T(8,128)S(1)}, f32[5,1,1024]{2,0,1:T(8,128)S(1)}, u32[]{:S(2)}, u32[]{:S(2)}) collective-permute-start(f32[5,1,1024]{2,0,1:T(8,128)S(1)} %get-tuple-element.15), channel_id=1, source_target_pairs={{0,4},{4,8},{8,12},{12,16},{16,20},{20,24},{24,28},{1,5},{5,9},{9,... | collective-permute-start | bytes 61448 | tf_op jit(solution)/shard_map/ppermute | solution.py:22
  14.9 0.9 fusion.25
  15.9 0.9 copy.84
  16.8 1.5 bitcast_bitcast_fusion.4
  18.3 4.4 %reshape.35 = f32[8,1,2560]{2,1,0:T(1,128)} reshape(f32[1024,4,5]{2,1,0:T(4,128)} %bitcast_bitcast_fusion.4) | data formatting | bytes 163840
  22.7 6.2 %all-to-all-start.1 = ((f32[8,1,2560]{2,1,0:T(1,128)}), f32[8,1,2560]{2,1,0:T(1,128)S(1)}, u32[]{:S(2)}, u32[]{:S(2)}) async-start(f32[8,1,2560]{2,1,0:T(1,128)} %reshape.35), calls=%async_computation.1 | async-start | bytes 163840 | tf_op jit(solution)/shard_map/all_to_all | solution.py:108
  28.9 1.7 copy.85
  30.6 1.8 bitcast_bitcast_fusion.3
  32.4 1.7 copy.87
  34.2 3.1 %bitcast_bitcast_fusion.1 = f32[1024,4,5]{2,1,0:T(4,128)} fusion(f32[1,5,4,1024]{1,2,3,0:T(4,128)} %copy.87), kind=kLoop, calls=%fused_computation.140 | loop fusion | bytes 163840
  37.2 1.7 copy.88
  38.9 3.1 %bitcast_bitcast_fusion = f32[1024,4,5]{2,1,0:T(4,128)} fusion(f32[1,5,4,1024]{1,2,3,0:T(4,128)} %copy.88), kind=kLoop, calls=%fused_computation.139 | loop fusion | bytes 163840
  42.0 1.7 copy.86
  43.7 3.1 %bitcast_bitcast_fusion.2 = f32[1024,4,5]{2,1,0:T(4,128)} fusion(f32[1,5,4,1024]{1,2,3,0:T(4,128)} %copy.86), kind=kLoop, calls=%fused_computation.141 | loop fusion | bytes 163840
  46.8 2.9 %reshape.37 = f32[8,1,2560]{2,1,0:T(1,128)} reshape(f32[1024,4,5]{2,1,0:T(4,128)S(1)} %bitcast_bitcast_fusion.3) | data formatting | bytes 163840
  49.8 4.5 %reshape.39 = f32[8,1,2560]{2,1,0:T(1,128)} reshape(f32[1024,4,5]{2,1,0:T(4,128)} %bitcast_bitcast_fusion.1) | data formatting | bytes 163840
  54.3 2.9 %reshape.41 = f32[8,1,2560]{2,1,0:T(1,128)} reshape(f32[1024,4,5]{2,1,0:T(4,128)S(1)} %copy-done.2) | data formatting | bytes 163840
  57.2 4.4 %reshape.31 = f32[8,1,2560]{2,1,0:T(1,128)} reshape(f32[1024,4,5]{2,1,0:T(4,128)} %bitcast_bitcast_fusion.2) | data formatting | bytes 163840
  61.7 0.3 fusion.2
  62.0 6.0 %all-to-all-start.2 = ((f32[8,1,2560]{2,1,0:T(1,128)}), f32[8,1,2560]{2,1,0:T(1,128)S(1)}, u32[]{:S(2)}, u32[]{:S(2)}) async-start(f32[8,1,2560]{2,1,0:T(1,128)} %reshape.37), calls=%async_computation.2 | async-start | bytes 163840 | tf_op jit(solution)/shard_map/all_to_all | solution.py:109
  68.0 0.2 convolution_bitcast_fusion
  68.2 0.9 copy.65
  69.1 2.9 %reshape.33 = f32[8,1,2560]{2,1,0:T(1,128)} reshape(f32[1024,4,5]{2,1,0:T(4,128)S(1)} %bitcast.94) | data formatting | bytes 163840
  72.0 0.5 broadcast.105
  72.5 0.8 reduce.5
  73.4 3.9 %reshape.36 = f32[1024,4,5]{2,1,0:T(4,128)} reshape(f32[8,2560]{1,0:T(8,128)S(1)} %reduce.5) | data formatting | bytes 163840
  77.3 6.0 %all-to-all-start.4 = ((f32[8,1,2560]{2,1,0:T(1,128)}), f32[8,1,2560]{2,1,0:T(1,128)S(1)}, u32[]{:S(2)}, u32[]{:S(2)}) async-start(f32[8,1,2560]{2,1,0:T(1,128)} %reshape.39), calls=%async_computation.4 | async-start | bytes 163840 | tf_op jit(solution)/shard_map/all_to_all | solution.py:111
  83.3 2.0 bitcast_negate_fusion.3
  85.3 0.8 reduce.6
  86.2 3.9 %reshape.38 = f32[1024,4,5]{2,1,0:T(4,128)} reshape(f32[8,2560]{1,0:T(8,128)S(1)} %reduce.6) | data formatting | bytes 163840
  90.1 0.2 all-to-all-done.4
  90.3 5.8 %all-to-all-start.5 = ((f32[8,1,2560]{2,1,0:T(1,128)}), f32[8,1,2560]{2,1,0:T(1,128)S(1)}, u32[]{:S(2)}, u32[]{:S(2)}) async-start(f32[8,1,2560]{2,1,0:T(1,128)} %reshape.41), calls=%async_computation.5 | async-start | bytes 163840 | tf_op jit(solution)/shard_map/all_to_all | solution.py:112
  96.1 3.4 %bitcast_negate_fusion.2 = f32[5,4,1024]{0,1,2:T(4,128)} fusion(f32[1024,4,5]{2,1,0:T(4,128)} %reshape.38), kind=kLoop, calls=%fused_computation.137 | loop fusion | flops 20480 | bytes 163840 | tf_op jit(solution)/shard_map/neg | solution.py:42
  99.5 0.8 reduce.3
  100.4 3.9 %reshape.40 = f32[1024,4,5]{2,1,0:T(4,128)} reshape(f32[8,2560]{1,0:T(8,128)S(1)} %reduce.3) | data formatting | bytes 163840
  104.2 6.0 %all-to-all-start.3 = ((f32[8,1,2560]{2,1,0:T(1,128)}), f32[8,1,2560]{2,1,0:T(1,128)S(1)}, u32[]{:S(2)}, u32[]{:S(2)}) async-start(f32[8,1,2560]{2,1,0:T(1,128)} %reshape.31), calls=%async_computation.3 | async-start | bytes 163840 | tf_op jit(solution)/shard_map/all_to_all | solution.py:110
  110.2 3.3 %bitcast_negate_fusion.1 = f32[5,4,1024]{0,1,2:T(4,128)} fusion(f32[1024,4,5]{2,1,0:T(4,128)} %reshape.40), kind=kLoop, calls=%fused_computation.136 | loop fusion | flops 20480 | bytes 163840 | tf_op jit(solution)/shard_map/neg | solution.py:49
  113.6 0.8 reduce.1
  114.4 3.9 %reshape.42 = f32[1024,4,5]{2,1,0:T(4,128)} reshape(f32[8,2560]{1,0:T(8,128)S(1)} %reduce.1) | data formatting | bytes 163840
  118.4 6.0 %all-to-all-start = ((f32[8,1,2560]{2,1,0:T(1,128)}), f32[8,1,2560]{2,1,0:T(1,128)S(1)}, u32[]{:S(2)}, u32[]{:S(2)}) async-start(f32[8,1,2560]{2,1,0:T(1,128)} %reshape.33), calls=%async_computation | async-start | bytes 163840 | tf_op jit(solution)/shard_map/all_to_all | solution.py:107
  124.4 3.4 %bitcast_negate_fusion = f32[5,4,1024]{0,1,2:T(4,128)} fusion(f32[1024,4,5]{2,1,0:T(4,128)} %reshape.42), kind=kLoop, calls=%fused_computation.135 | loop fusion | flops 20480 | bytes 163840 | tf_op jit(solution)/shard_map/neg | solution.py:50
  127.8 0.8 copy.69
  128.6 2.0 copy.71
  130.9 0.8 copy.75
  131.7 1.9 copy.77
  133.6 0.9 reduce.2
  134.5 2.6 reshape.32
  137.1 0.8 copy.73
  137.9 0.8 reduce.4
  138.8 2.6 reshape.34
  141.4 0.7 copy.83
  143.3 0.1 pad.116
  146.1 0.1 pad.136
  147.3 0.7 copy.78
  148.0 6.0 %all-to-all-start.6 = ((f32[5,32,128]{2,0,1:T(8,128)}), f32[5,32,128]{2,0,1:T(8,128)S(1)}, u32[]{:S(2)}, u32[]{:S(2)}) async-start(f32[5,32,128]{2,0,1:T(8,128)} %copy.78), calls=%async_computation.6 | async-start | bytes 262144 | tf_op jit(solution)/shard_map/all_to_all | solution.py:115
  154.1 22.6 %scatter_custom_fusion = f32[65536]{0:T(1024)} fusion(s32[4096]{0:T(1024)S(1)} %bitcast.115, f32[4096]{0:T(1024)S(1)} %bitcast.114, f32[]{:T(128)} %constant.9.clone.1), kind=kCustom, calls=%fused_computation.11 | custom fusion | flops 4096 | bytes 262148 | tf_op jit(solution)/shard_map/scatter-add | solution.py:87
  176.7 0.6 dynamic-slice
  177.9 32.6 %all-reduce.39.cloned.1.call-done = f32[65536]{0:T(1024)} async-done(((f32[65536]{0:T(1024)}), f32[65536]{0:T(1024)}) %all-reduce.39.cloned.1.call-update) | async-done | bytes 262160
  210.5 1.5 dynamic-slice.1
  212.0 0.9 multiply_reduce_fusion
  212.9 39.5 %psum.7 = f32[]{:T(128)} all-reduce(f32[]{:T(128)} %get-tuple-element.76), channel_id=1, replica_groups=mesh['stream'=8,'cross'=4] {'stream','cross'}, use_global_device_ids=true, to_apply=%region_1.0 | all-reduce | flops 1 | bytes 8 | tf_op jit(solution)/shard_map/psum | solution.py:117
  253.2 0.7 copy.82
  (257 shorter events, 4.7 us)
Async XLA Ops:
  7.2 204.9 %copy-start = (f32[5,5]{1,0:T(8,128)S(1)}, f32[5,5]{1,0:T(8,128)}, u32[]{:S(2)}) copy-start(f32[5,5]{1,0:T(8,128)} %param.16) | copy-start | bytes 304
  8.1 53.5 %collective-permute-start = (f32[5,1,1024]{2,0,1:T(8,128)S(1)}, f32[5,1,1024]{2,0,1:T(8,128)S(1)}, u32[]{:S(2)}, u32[]{:S(2)}) collective-permute-start(f32[5,1,1024]{2,0,1:T(8,128)S(1)} %get-tuple-element.16), channel_id=1, source_target_pairs={{4,0},{8,4},{12,8},{16,12},{20,16},{24,20},{28,24},{5,1},{9,5},{13... | collective-permute-start | bytes 61448 | tf_op jit(solution)/shard_map/ppermute | solution.py:23
  9.4 52.2 %collective-permute-start.1 = (f32[5,1,1024]{2,0,1:T(8,128)S(1)}, f32[5,1,1024]{2,0,1:T(8,128)S(1)}, u32[]{:S(2)}, u32[]{:S(2)}) collective-permute-start(f32[5,1,1024]{2,0,1:T(8,128)S(1)} %get-tuple-element.15), channel_id=1, source_target_pairs={{0,4},{4,8},{8,12},{12,16},{16,20},{20,24},{24,28},{1,5},{5,9},{9,... | collective-permute-start | bytes 61448 | tf_op jit(solution)/shard_map/ppermute | solution.py:22
  22.7 39.3 %all-to-all-start.1 = ((f32[8,1,2560]{2,1,0:T(1,128)}), f32[8,1,2560]{2,1,0:T(1,128)S(1)}, u32[]{:S(2)}, u32[]{:S(2)}) async-start(f32[8,1,2560]{2,1,0:T(1,128)} %reshape.35), calls=%async_computation.1 | async-start | bytes 163840 | tf_op jit(solution)/shard_map/all_to_all | solution.py:108
  30.6 1.8 copy-start.4
  49.8 4.5 %copy-start.2 = (f32[1024,4,5]{2,1,0:T(4,128)S(1)}, f32[1024,4,5]{2,1,0:T(4,128)}, u32[]{:S(2)}) copy-start(f32[1024,4,5]{2,1,0:T(4,128)} %bitcast_bitcast_fusion) | copy-start | bytes 245764
  54.3 7.4 %copy-start.5 = (f32[5,4,1024]{2,1,0:T(4,128)S(1)}, f32[5,4,1024]{2,1,0:T(4,128)}, u32[]{:S(2)}) copy-start(f32[5,4,1024]{2,1,0:T(4,128)} %param.10) | copy-start | bytes 245764
  54.3 7.4 %copy-start.8 = (f32[5,5]{1,0:T(8,128)S(1)}, f32[5,5]{1,0:T(8,128)}, u32[]{:S(2)}) copy-start(f32[5,5]{1,0:T(8,128)} %param.14) | copy-start | bytes 304
  54.3 13.7 %copy-start.9 = (f32[5,5]{1,0:T(8,128)S(1)}, f32[5,5]{1,0:T(8,128)}, u32[]{:S(2)}) copy-start(f32[5,5]{1,0:T(8,128)} %param.15) | copy-start | bytes 304
  62.0 15.3 %all-to-all-start.2 = ((f32[8,1,2560]{2,1,0:T(1,128)}), f32[8,1,2560]{2,1,0:T(1,128)S(1)}, u32[]{:S(2)}, u32[]{:S(2)}) async-start(f32[8,1,2560]{2,1,0:T(1,128)} %reshape.37), calls=%async_computation.2 | async-start | bytes 163840 | tf_op jit(solution)/shard_map/all_to_all | solution.py:109
  77.3 13.0 %all-to-all-start.4 = ((f32[8,1,2560]{2,1,0:T(1,128)}), f32[8,1,2560]{2,1,0:T(1,128)S(1)}, u32[]{:S(2)}, u32[]{:S(2)}) async-start(f32[8,1,2560]{2,1,0:T(1,128)} %reshape.39), calls=%async_computation.4 | async-start | bytes 163840 | tf_op jit(solution)/shard_map/all_to_all | solution.py:111
  90.3 13.9 %all-to-all-start.5 = ((f32[8,1,2560]{2,1,0:T(1,128)}), f32[8,1,2560]{2,1,0:T(1,128)S(1)}, u32[]{:S(2)}, u32[]{:S(2)}) async-start(f32[8,1,2560]{2,1,0:T(1,128)} %reshape.41), calls=%async_computation.5 | async-start | bytes 163840 | tf_op jit(solution)/shard_map/all_to_all | solution.py:112
  104.2 14.1 %all-to-all-start.3 = ((f32[8,1,2560]{2,1,0:T(1,128)}), f32[8,1,2560]{2,1,0:T(1,128)S(1)}, u32[]{:S(2)}, u32[]{:S(2)}) async-start(f32[8,1,2560]{2,1,0:T(1,128)} %reshape.31), calls=%async_computation.3 | async-start | bytes 163840 | tf_op jit(solution)/shard_map/all_to_all | solution.py:110
  118.4 19.6 %all-to-all-start = ((f32[8,1,2560]{2,1,0:T(1,128)}), f32[8,1,2560]{2,1,0:T(1,128)S(1)}, u32[]{:S(2)}, u32[]{:S(2)}) async-start(f32[8,1,2560]{2,1,0:T(1,128)} %reshape.33), calls=%async_computation | async-start | bytes 163840 | tf_op jit(solution)/shard_map/all_to_all | solution.py:107
  128.6 2.3 copy-start.1
  145.2 8.8 %copy-start.3 = (f32[5,4,1024]{2,1,0:T(4,128)S(1)}, f32[5,4,1024]{2,1,0:T(4,128)}, u32[]{:S(2)}) copy-start(f32[5,4,1024]{2,1,0:T(4,128)} %param.9) | copy-start | bytes 245764
  145.2 8.8 %copy-start.6 = (f32[5,4,1024]{2,1,0:T(4,128)S(1)}, f32[5,4,1024]{2,1,0:T(4,128)}, u32[]{:S(2)}) copy-start(f32[5,4,1024]{2,1,0:T(4,128)} %param.11) | copy-start | bytes 245764
  145.5 8.5 %copy-start.7 = (s32[4,1024]{1,0:T(4,128)S(1)}, s32[4,1024]{1,0:T(4,128)}, u32[]{:S(2)}) copy-start(s32[4,1024]{1,0:T(4,128)} %param.17) | copy-start | bytes 49156
  146.0 30.7 %copy-start.10 = (u32[32]{0:T(128)S(1)}, u32[32]{0:T(128)}, u32[]{:S(2)}) copy-start(u32[32]{0:T(128)} %constant.98) | copy-start | bytes 388
  148.0 64.0 %all-to-all-start.6 = ((f32[5,32,128]{2,0,1:T(8,128)}), f32[5,32,128]{2,0,1:T(8,128)S(1)}, u32[]{:S(2)}, u32[]{:S(2)}) async-start(f32[5,32,128]{2,0,1:T(8,128)} %copy.78), calls=%async_computation.6 | async-start | bytes 262144 | tf_op jit(solution)/shard_map/all_to_all | solution.py:115
  154.0 56.5 %all-reduce.39.cloned.1.call-start = ((), (), s32[]{:S(2)}) async-start(), calls=%async_computation.7 | async-start | bytes 524288
Sparse Core Ops, SparseCore 0:
  176.8 33.6 all-reduce.38
where the time goes:
time: 262 us; the launch traced here: 261 us
  local copies, waits for them, and re-layouts  81 us (31%)
  starting transfers between devices  48.9 us (19%)
  other arithmetic  40.6 us (15%)
  blocking collectives  39.5 us (15%)
  waiting for transfers between devices  32.8 us (13%)
  between operations  16.5 us (6%)
    unnamed x52, local copies, waits for them, and re-layouts  67 us
    psum x1, blocking collectives, shards(): squares = lax.psum(jnp.sum(increment * increment), ('stream', 'cross'))  39.5 us
    unnamed x2, waiting for transfers between devices  32.6 us
    scatter-add x1, other arithmetic, shards(): jax.ops.segment_sum(contribution.ravel(), ctrl_local.ravel(), num_segment...  22.6 us
    all_to_all x1, starting transfers between devices, shards(): lax.all_to_all(packed[1], 'stream', split_axis=2, concat_axis=1, tiled=True)  6.22 us
    all_to_all x1, starting transfers between devices, shards(): lax.all_to_all(packed[2], 'stream', split_axis=2, concat_axis=1, tiled=True)  6.01 us
    all_to_all x1, starting transfers between devices, shards(): lax.all_to_all(packed[0], 'stream', split_axis=2, concat_axis=1, tiled=True)  6 us
    all_to_all x1, starting transfers between devices, shards(): lax.all_to_all(packed[3], 'stream', split_axis=2, concat_axis=1, tiled=True)  6 us
  transfers between devices with their start and end apart: 10, of which 2 were waited for; matrix products, arithmetic and copies ran while one was open for 43% of the time, Pallas kernels for 0%

commit v1 on v0

v1 whole, which is shorter than its diff:
```python
import functools

import jax
import jax.numpy as jnp
from jax import lax
from jax.experimental import pallas as pl
from jax.experimental.pallas import tpu as pltpu
from jax.sharding import PartitionSpec as P

NCTRL = 524288
LANES = 128
SUBLANES = 8

dissipation = 0.25
step_scale = 0.5
epsilon = 1e-06

VMEM = pl.BlockSpec(memory_space=pltpu.VMEM)
SMEM = pl.BlockSpec(memory_space=pltpu.SMEM)


def round_up(value, step):
    return -(-value // step) * step


def mix(matrix_ref, columns):
    count = len(columns)
    return [
        sum(matrix_ref[f, g] * columns[g] for g in range(1, count)) + matrix_ref[f, 0] * columns[0]
        for f in range(count)
    ]


CELL_KINDS = 5


def block_rows(fields, cells):
    return round_up(fields * (CELL_KINDS * cells + cells - 1 + 2), SUBLANES)


def pack_kernel(parts, width, jac, left, adj, src, low, up, out, pad):
    fields, cells, length = adj.shape
    rows = block_rows(fields, cells)
    if width < LANES or rows > fields * (CELL_KINDS * cells + cells + 1):
        out[...] = jnp.zeros_like(out)
    pad[...] = jnp.zeros_like(pad)
    for f in range(fields):
        pad[f, 1 : cells + 1, :] = adj[f]
    ahead = [pad[f, 2 : cells + 2, :] for f in range(fields)]
    behind = [pad[f, 0:cells, :] for f in range(fields)]
    central = mix(jac, [a - b for a, b in zip(ahead, behind)])
    residual = [
        src[f] - 0.5 * central[f] + dissipation * (ahead[f] - 2.0 * adj[f] + behind[f])
        for f in range(fields)
    ]
    characteristic = mix(left, residual)
    cell = lax.broadcasted_iota(jnp.int32, (cells, length), 0)
    extra = CELL_KINDS * fields * cells
    for f in range(fields):
        diagonal = up[0, f]
        inverse = 1.0 / diagonal
        own = jnp.where(cell == 1, inverse, 1.0)
        diagonal_1 = jnp.broadcast_to(up[0, f, 1:2, :], (cells, length))
        values = (
            characteristic[f] * own,
            low[0, f] * jnp.where(cell == 2, diagonal_1, own),
            low[1, f] * jnp.where(cell == 3, diagonal_1, own),
            up[1, f] * inverse,
            up[2, f] * inverse,
        )
        for d in range(parts):
            lanes = slice(d * width, (d + 1) * width)
            for k, value in enumerate(values):
                at = (k * fields + f) * cells
                out[d, at : at + cells, 0:width] = value[:, lanes]
            at = extra + f * (cells + 1)
            out[d, at : at + 1, 0:width] = inverse[0:1, lanes]
            out[d, at + 1 : at + cells - 1, 0:width] = inverse[2:cells, lanes]
            out[d, at + cells - 1 : at + cells, 0:width] = adj[f, 0:1, lanes]
            out[d, at + cells : at + cells + 1, 0:width] = adj[f, cells - 1 : cells, lanes]


def solve_kernel(parts, fields, cells, jac, left, right, lines, out, edge, whole):
    rows = block_rows(fields, cells)
    back = round_up(fields * cells + 1, SUBLANES)
    extra = CELL_KINDS * fields * cells

    def across(row):
        return lines[pl.ds(row, parts, stride=rows), :]

    firsts = [across(extra + f * (cells + 1) + cells - 1) for f in range(fields)]
    lasts = [across(extra + f * (cells + 1) + cells) for f in range(fields)]
    from_last = mix(jac, lasts)
    from_first = mix(jac, firsts)
    into_first = mix(left, [0.5 * a + dissipation * b for a, b in zip(from_last, lasts)])
    into_last = mix(left, [dissipation * b - 0.5 * a for a, b in zip(from_first, firsts)])
    for f in range(fields):
        edge[f * parts : (f + 1) * parts, :] = into_first[f]
        edge[(fields + f) * parts : (fields + f + 1) * parts, :] = into_last[f]

    def kind(d, k, i):
        return lines[pl.ds(d * rows + k * fields * cells + i, fields, stride=cells), :]

    def inverse(d, i):
        at = d * rows + extra + (i if i == 0 else i - 1)
        return lines[pl.ds(at, fields, stride=cells + 1), :]

    forward = {}
    one = two = None
    for d in range(parts):
        for i in range(cells):
            value = kind(d, 0, i)
            if i == 0 and d > 0:
                value = value + edge[pl.ds(d - 1, fields, stride=parts), :]
            if i == cells - 1 and d < parts - 1:
                value = value + edge[pl.ds(fields * parts + d + 1, fields, stride=parts), :]
            if two is not None:
                value = value - kind(d, 2, i) * two
            if one is not None:
                value = value - kind(d, 1, i) * one
            forward[d, i] = value
            one, two = value, one
    one = two = None
    total = parts * cells
    for d in reversed(range(parts)):
        for i in reversed(range(cells)):
            value = forward[d, i] if i == 1 else forward[d, i] * inverse(d, i)
            if two is not None:
                value = value - kind(d, 4, i) * two
            if one is not None:
                value = value - kind(d, 3, i) * one
            whole[pl.ds(d * cells + i, fields, stride=total), :] = value
            one, two = value, one
    increment = mix(right, [whole[g * total : (g + 1) * total, :] for g in range(fields)])
    squares = sum(v * v for v in increment[1:]) + increment[0] * increment[0]
    squares = jnp.broadcast_to(jnp.sum(squares, axis=0, keepdims=True), (back - fields * cells, LANES))
    for d in range(parts):
        for f in range(fields):
            at = d * back + f * cells
            out[at : at + cells, :] = increment[f][d * cells : (d + 1) * cells, :]
        out[d * back + fields * cells : (d + 1) * back, :] = squares


def slab_kernel(peers, me, adj, grad, ctrl, *outs):
    fields, cells, length = adj.shape
    height = outs[0].shape[0]
    contribution = adj[0] * grad[0]
    for f in range(1, fields):
        contribution = contribution + adj[f] * grad[f]
    upper = contribution.astype(jnp.bfloat16).astype(jnp.float32)
    lower = contribution - upper
    high = lax.shift_right_logical(ctrl[...], 7)
    low = lax.bitwise_and(ctrl[...], LANES - 1)
    block = lax.broadcasted_iota(jnp.int32, (height, length), 0)
    lane = lax.broadcasted_iota(jnp.int32, (LANES, length), 0)
    sums = None
    for i in range(cells):
        hit = lane == low[i : i + 1, :]
        terms = jnp.concatenate(
            [
                jnp.where(hit, upper[i : i + 1, :], 0.0).astype(jnp.bfloat16),
                jnp.where(hit, lower[i : i + 1, :], 0.0).astype(jnp.bfloat16),
            ],
            axis=0,
        )
        rows = []
        for k in range(peers):
            offset = lax.bitwise_xor(me[0], k) * height
            rows.append(jnp.where(block == high[i : i + 1, :] - offset, 1.0, 0.0).astype(jnp.bfloat16))
        picked = jnp.concatenate(rows, axis=0)
        part = lax.dot_general(
            picked, terms, (((1,), (1,)), ((), ())), preferred_element_type=jnp.float32
        )
        sums = part if sums is None else sums + part
    sums = sums[:, :LANES] + sums[:, LANES:]
    for k in range(peers):
        outs[k][...] = sums[k * height : (k + 1) * height, :]


def finish_kernel(parts, width, peers, cell_count, adj, moved, *refs):
    squares, blocks, (out, sens) = refs[:peers], refs[peers : 2 * peers], refs[2 * peers :]
    fields, cells, _ = adj.shape
    back = moved.shape[0] // parts
    total = squares[0][...]
    slab = blocks[0][...]
    for k in range(1, peers):
        total = total + squares[k][...]
        slab = slab + blocks[k][...]
    sens[...] = slab
    total = jnp.sum(jnp.sum(total, axis=0, keepdims=True), axis=1, keepdims=True)
    factor = step_scale / jnp.sqrt(total / cell_count + epsilon)
    for d in range(parts):
        lanes = slice(d * width, (d + 1) * width)
        for f in range(fields):
            at = d * back + f * cells
            out[f, :, lanes] = adj[f, :, lanes] + factor * moved[at : at + cells, 0:width]


def shards(
    adjoint, source, shape_grad, lower_band, upper_band, jacobian, left_vectors, right_vectors, ctrl_local
):
    fields, cells, length = adjoint.shape
    parts, peers = lax.axis_size("stream"), lax.axis_size("cross")
    width = length // parts
    rows = block_rows(fields, cells)
    back = round_up(fields * cells + 1, SUBLANES)
    f32 = jnp.float32

    packed = pl.pallas_call(
        functools.partial(pack_kernel, parts, width),
        out_shape=jax.ShapeDtypeStruct((parts, rows, LANES), f32),
        in_specs=[SMEM, SMEM, VMEM, VMEM, VMEM, VMEM],
        out_specs=VMEM,
        scratch_shapes=[pltpu.VMEM((fields, round_up(cells + 2, SUBLANES), length), f32)],
        name="pack",
    )(jacobian, left_vectors, adjoint, source, lower_band, upper_band)
    lines = lax.all_to_all(
        packed.reshape(parts * rows, LANES), "stream", split_axis=0, concat_axis=0, tiled=True
    )

    height = NCTRL // (parts * peers * LANES)
    me = lax.axis_index("cross").astype(jnp.int32).reshape(1)
    blocks = pl.pallas_call(
        functools.partial(slab_kernel, peers),
        out_shape=[jax.ShapeDtypeStruct((height, LANES), f32)] * peers,
        in_specs=[SMEM, VMEM, VMEM, VMEM],
        out_specs=[VMEM] * peers,
        cost_estimate=pl.CostEstimate(
            flops=4 * cells * length * NCTRL // parts, bytes_accessed=4 << 20, transcendentals=0
        ),
        name="slab",
    )(me, adjoint, shape_grad, ctrl_local)

    def exchange(arrays):
        return [arrays[0]] + [
            lax.ppermute(arrays[k], "cross", [(i, i ^ k) for i in range(peers)])
            for k in range(1, peers)
        ]

    blocks = exchange(blocks)

    moved = pl.pallas_call(
        functools.partial(solve_kernel, parts, fields, cells),
        out_shape=jax.ShapeDtypeStruct((parts * back, LANES), f32),
        in_specs=[SMEM, SMEM, SMEM, VMEM],
        out_specs=VMEM,
        scratch_shapes=[
            pltpu.VMEM((2 * fields * parts, LANES), f32),
            pltpu.VMEM((fields * parts * cells, LANES), f32),
        ],
        name="solve",
    )(jacobian, left_vectors, right_vectors, lines)
    moved = lax.all_to_all(moved, "stream", split_axis=0, concat_axis=0, tiled=True)
    squares = moved.reshape(parts, back, LANES)[:, fields * cells, :]
    squares = exchange([squares] * peers)

    cell_count = fields * cells * length * parts * peers
    adjoint_next, sensitivity = pl.pallas_call(
        functools.partial(finish_kernel, parts, width, peers, cell_count),
        out_shape=[
            jax.ShapeDtypeStruct(adjoint.shape, f32),
            jax.ShapeDtypeStruct((height, LANES), f32),
        ],
        in_specs=[VMEM] * (2 + 2 * peers),
        out_specs=[VMEM, VMEM],
        name="finish",
    )(adjoint, moved, *squares, *blocks)
    return adjoint_next, sensitivity.reshape(height * LANES)


def solution(mesh):
    in_specs = (
        P(None, "stream", "cross"),
        P(None, "stream", "cross"),
        P(None, "stream", "cross"),
        P(None, None, "stream", "cross"),
        P(None, None, "stream", "cross"),
        P(),
        P(),
        P(),
        P("stream", "cross"),
    )
    out_specs = (P(None, "stream", "cross"), P(("stream", "cross")))
    return jax.shard_map(shards, mesh=mesh, in_specs=in_specs, out_specs=out_specs, check_vma=False)
```

time: 262 us -> 44.9 us (0.17)
  local copies, waits for them, and re-layouts: 81 us -> 0.58 us
  starting transfers between devices: 48.9 us -> 7.37 us
  other arithmetic: 40.6 us -> 0 us
  waiting for transfers between devices: 32.8 us -> 4.95 us
  blocking collectives: 39.5 us -> 21.9 us
  between operations: 16.5 us -> 0.72 us
  Pallas kernels: 0 us -> 9.01 us
    unnamed x52 -> x16, local copies, waits for them, and re-layouts: 67 us -> 0.57 us
    psum x1 -> x0, blocking collectives: 39.5 us -> none  [shards(): squares = lax.psum(jnp.sum(increment * increment), ('stream', 'cross'))]
    all_to_all x7 -> x1, starting transfers between devices: 42 us -> 3.59 us  [shards(): lax.all_to_all(moved, 'stream', split_axis=0, concat_axis=0, tiled=True)]
    unnamed x2 -> x0, waiting for transfers between devices: 32.6 us -> none
    scatter-add x1 -> x0, other arithmetic: 22.6 us -> none  [shards(): jax.ops.segment_sum(contribution.ravel(), ctrl_local.ravel(), num_segment...]
    all_to_all x0 -> x1, blocking collectives: none -> 21.9 us  [shards(): lax.all_to_all(packed.reshape(parts * rows, LANES), 'stream', split_axis=...]
    neg x4 -> x0, other arithmetic: 12.2 us -> none  [the longest x2 5.43 us: forward_maps(): return (-first_sub, -second_sub, unit_fill, zero_fill, rhs_cells, zero_fill)]
    pallas_call x0 -> x4, Pallas kernels: none -> 9.01 us  [the longest x1 3.05 us: shards(): pl.pallas_call(functools.partial(slab_kernel, peers), out_shape=[jax.Shap...]
  transfers between devices with their start and end apart: 10 -> 7, of which waited for: 2 -> 3; matrix products, arithmetic and copies ran while one was open for 43% -> 0% of each run, Pallas kernels for 0% -> 7%
where the time goes in v1:
time: 44.9 us; the launch traced here: 44.5 us
  blocking collectives  21.9 us (49%)
  Pallas kernels  9.01 us (20%)
  starting transfers between devices  7.37 us (16%)
  waiting for transfers between devices  4.95 us (11%)
  between operations  0.72 us (2%)
  local copies, waits for them, and re-layouts  0.58 us (1%)
    all_to_all x1, blocking collectives, shards(): lax.all_to_all(packed.reshape(parts * rows, LANES), 'stream', split_axis=...  21.9 us
    ppermute x6, starting transfers between devices, exchange(): lax.ppermute(arrays[k], 'cross', [(i, i ^ k) for i in range(peers)])  3.78 us
    all_to_all x1, starting transfers between devices, shards(): lax.all_to_all(moved, 'stream', split_axis=0, concat_axis=0, tiled=True)  3.59 us
    pallas_call x1, Pallas kernels, shards(): pl.pallas_call(functools.partial(slab_kernel, peers), out_shape=[jax.Shap...  3.05 us
    ppermute x6, waiting for transfers between devices, exchange(): lax.ppermute(arrays[k], 'cross', [(i, i ^ k) for i in range(peers)])  2.74 us
    pallas_call x1, Pallas kernels, shards(): pl.pallas_call(functools.partial(pack_kernel, parts, width), out_shape=ja...  2.24 us
    all_to_all x1, waiting for transfers between devices, shards(): lax.all_to_all(moved, 'stream', split_axis=0, concat_axis=0, tiled=True)  2.21 us
    pallas_call x1, Pallas kernels, shards(): pl.pallas_call(functools.partial(solve_kernel, parts, fields, cells), out...  1.92 us
  transfers between devices with their start and end apart: 7, of which 3 were waited for; matrix products, arithmetic and copies ran while one was open for 0% of the time, Pallas kernels for 7%

profile of v1, /device:TPU:0, one launch (start us, length us, event | category | flops | bytes accessed | tf_op | source)
XLA Modules:
  0.0 44.5 jit_solution(2667686347034421309)
XLA Ops:
  0.6 2.2 %pack.1 = f32[8,128,128]{2,1,0:T(8,128)} custom-call(f32[5,5]{1,0:T(8,128)} %jac.3, f32[5,5]{1,0:T(8,128)} %left.3, f32[5,4,1024]{2,1,0:T(4,128)} %adj.5, f32[5,4,1024]{2,1,0:T(4,128)} %src.1, f32[2,5,4,1024]{3,2,1,0:T(4,128)} %low.1, f32[3,5,4,1024]{3,2,1,0:T(4,128)} %up.1), custom_call_target="tpu_custom_call" | custom-call | tf_op jit(solution)/shard_map/pack/pallas_call | solution.py:209
  2.9 21.9 %all_to_all.19 = f32[8,128,128]{2,1,0:T(8,128)} all-to-all(f32[8,128,128]{2,1,0:T(8,128)} %pack.1), channel_id=1, replica_groups=mesh['stream'=8,'cross'=4] {'stream'}, dimensions={0} | all-to-all | bytes 1048576 | tf_op jit(solution)/shard_map/all_to_all | solution.py:217
  24.8 1.9 %solve.1 = f32[192,128]{1,0:T(8,128)} custom-call(f32[5,5]{1,0:T(8,128)} %jac.3, f32[5,5]{1,0:T(8,128)} %left.3, f32[5,5]{1,0:T(8,128)} %right.1, f32[1024,128]{1,0:T(8,128)} %bitcast.8), custom_call_target="tpu_custom_call" | custom-call | tf_op jit(solution)/shard_map/solve/pallas_call | solution.py:242
  26.7 3.6 %all-to-all-start.1 = ((f32[8,24,128]{2,1,0:T(8,128)}), f32[8,24,128]{2,1,0:T(8,128)S(1)}, u32[]{:S(2)}, u32[]{:S(2)}) async-start(f32[8,24,128]{2,1,0:T(8,128)} %bitcast.10), calls=%async_computation.1 | async-start | bytes 196608 | tf_op jit(solution)/shard_map/all_to_all | solution.py:253
  30.3 3.0 %slab.1 = (f32[128,128]{1,0:T(8,128)}, f32[128,128]{1,0:T(8,128)}, f32[128,128]{1,0:T(8,128)}, f32[128,128]{1,0:T(8,128)}) custom-call(s32[1]{0:T(128)} %bitcast.4.me, f32[5,4,1024]{2,1,0:T(4,128)} %adj.5, f32[5,4,1024]{2,1,0:T(4,128)} %grad.1, s32[4,1024]{1,0:T(4,128)} %ctrl.1), custom_call_target="tpu_custom_call" | custom-call | flops 1073741824 | bytes 4194304 | tf_op jit(solution)/shard_map/slab/pallas_call | solution.py:223
  33.3 0.0 collective-permute-start.3
  33.3 1.5 %collective-permute-start.4 = (f32[128,128]{1,0:T(8,128)}, f32[128,128]{1,0:T(8,128)S(1)}, u32[]{:S(2)}, u32[]{:S(2)}) collective-permute-start(f32[128,128]{1,0:T(8,128)} %get-tuple-element.10), channel_id=1, source_target_pairs={{0,2},{1,3},{2,0},{3,1},{4,6},{5,7},{6,4},{7,5},{8,10},{9,11},{10,... | collective-permute-start | bytes 196616 | tf_op jit(solution)/shard_map/ppermute | solution.py:236
  34.9 0.3 collective-permute-start.5
  35.2 2.2 %all-to-all-done.1 = f32[8,24,128]{2,1,0:T(8,128)S(1)} async-done(((f32[8,24,128]{2,1,0:T(8,128)}), f32[8,24,128]{2,1,0:T(8,128)S(1)}, u32[]{:S(2)}, u32[]{:S(2)}) %all-to-all-start.1) | async-done | bytes 98336 | tf_op jit(solution)/shard_map/all_to_all | solution.py:253
  37.4 0.0 copy-start
  37.4 0.0 copy-start.4
  37.4 0.1 collective-permute-start
  37.5 1.6 %collective-permute-start.1 = (f32[8,128]{1,0:T(8,128)S(1)}, f32[8,128]{1,0:T(8,128)S(1)}, u32[]{:S(2)}, u32[]{:S(2)}) collective-permute-start(f32[8,128]{1,0:T(8,128)S(1)} %bitcast.12), channel_id=1, source_target_pairs={{0,2},{1,3},{2,0},{3,1},{4,6},{5,7},{6,4},{7,5},{8,10},{9,11},{10,... | collective-permute-start | bytes 12296 | tf_op jit(solution)/shard_map/ppermute | solution.py:236
  39.1 0.0 collective-permute-done.3.refs_5_
  39.1 0.0 copy-start.1
  39.1 0.3 collective-permute-start.2
  39.4 0.0 collective-permute-done.4.refs_6_
  39.4 0.0 copy-start.2
  39.4 0.0 collective-permute-done.5.refs_7_
  39.4 0.0 copy-start.3
  39.4 0.0 collective-permute-done.refs_1_
  39.4 0.0 copy-start.5
  39.4 1.8 %collective-permute-done.1.refs_2_ = f32[8,128]{1,0:T(8,128)S(1)} collective-permute-done((f32[8,128]{1,0:T(8,128)S(1)}, f32[8,128]{1,0:T(8,128)S(1)}, u32[]{:S(2)}, u32[]{:S(2)}) %collective-permute-start.1) | collective-permute-done | bytes 4128 | tf_op jit(solution)/shard_map/ppermute | solution.py:236
  41.2 0.0 copy-start.6
  41.2 0.9 %collective-permute-done.2.refs_3_ = f32[8,128]{1,0:T(8,128)S(1)} collective-permute-done((f32[8,128]{1,0:T(8,128)S(1)}, f32[8,128]{1,0:T(8,128)S(1)}, u32[]{:S(2)}, u32[]{:S(2)}) %collective-permute-start.2) | collective-permute-done | bytes 4128 | tf_op jit(solution)/shard_map/ppermute | solution.py:236
  42.1 0.0 copy-start.7
  42.1 0.0 copy-done
  42.1 0.0 copy-done.4
  42.2 0.0 copy-done.1
  42.2 0.0 copy-done.2
  42.2 0.0 copy-done.3
  42.2 0.0 copy-done.5
  42.2 0.0 copy-done.6
  42.2 0.5 %copy-done.7 = f32[8,128]{1,0:T(8,128)} copy-done((f32[8,128]{1,0:T(8,128)}, f32[8,128]{1,0:T(8,128)S(1)}, u32[]{:S(2)}) %copy-start.7) | copy-done | bytes 4120
  42.7 1.8 %finish.1 = (f32[5,4,1024]{2,1,0:T(4,128)}, f32[128,128]{1,0:T(8,128)}) custom-call(f32[5,4,1024]{2,1,0:T(4,128)} %adj.5, f32[192,128]{1,0:T(8,128)} %bitcast.9, f32[8,128]{1,0:T(8,128)} %bitcast.14, f32[8,128]{1,0:T(8,128)} %copy-done.5, f32[8,128]{1,0:T(8,128)} %copy-done.6, f32[8,128]{1,0:T(8,128)} %copy-done.7, f32[128,128]{1,0:T(8,128)} %get-tuple-element.8.refs_4_, ...), custom_call_target="tpu_custom_call" | custom-call | tf_op jit(solution)/shard_map/finish/pallas_call | solution.py:258
  (1 shorter events, 0.0 us)
Async XLA Ops:
  26.7 10.7 %all-to-all-start.1 = ((f32[8,24,128]{2,1,0:T(8,128)}), f32[8,24,128]{2,1,0:T(8,128)S(1)}, u32[]{:S(2)}, u32[]{:S(2)}) async-start(f32[8,24,128]{2,1,0:T(8,128)} %bitcast.10), calls=%async_computation.1 | async-start | bytes 196608 | tf_op jit(solution)/shard_map/all_to_all | solution.py:253
  33.3 5.8 %collective-permute-start.3 = (f32[128,128]{1,0:T(8,128)}, f32[128,128]{1,0:T(8,128)S(1)}, u32[]{:S(2)}, u32[]{:S(2)}) collective-permute-start(f32[128,128]{1,0:T(8,128)} %get-tuple-element.9), channel_id=1, source_target_pairs={{0,1},{1,0},{2,3},{3,2},{4,5},{5,4},{6,7},{7,6},{8,9},{9,8},{10,11... | collective-permute-start | bytes 196616 | tf_op jit(solution)/shard_map/ppermute | solution.py:236
  33.3 6.0 %collective-permute-start.4 = (f32[128,128]{1,0:T(8,128)}, f32[128,128]{1,0:T(8,128)S(1)}, u32[]{:S(2)}, u32[]{:S(2)}) collective-permute-start(f32[128,128]{1,0:T(8,128)} %get-tuple-element.10), channel_id=1, source_target_pairs={{0,2},{1,3},{2,0},{3,1},{4,6},{5,7},{6,4},{7,5},{8,10},{9,11},{10,... | collective-permute-start | bytes 196616 | tf_op jit(solution)/shard_map/ppermute | solution.py:236
  34.9 4.5 %collective-permute-start.5 = (f32[128,128]{1,0:T(8,128)}, f32[128,128]{1,0:T(8,128)S(1)}, u32[]{:S(2)}, u32[]{:S(2)}) collective-permute-start(f32[128,128]{1,0:T(8,128)} %get-tuple-element.11), channel_id=1, source_target_pairs={{0,3},{1,2},{2,1},{3,0},{4,7},{5,6},{6,5},{7,4},{8,11},{9,10},{10,... | collective-permute-start | bytes 196616 | tf_op jit(solution)/shard_map/ppermute | solution.py:236
  37.4 4.7 %copy-start = (f32[8,24,128]{2,1,0:T(8,128)}, f32[8,24,128]{2,1,0:T(8,128)S(1)}, u32[]{:S(2)}) copy-start(f32[8,24,128]{2,1,0:T(8,128)S(1)} %all-to-all-done.1) | copy-start | bytes 294916
  37.4 4.7 %copy-start.4 = (f32[8,1,128]{2,1,0:T(1,128)}, f32[8,1,128]{2,1,0:T(1,128)S(1)}, u32[]{:S(2)}) copy-start(f32[8,1,128]{2,1,0:T(1,128)S(1)} %slice.4) | copy-start | bytes 12292
  37.4 2.0 %collective-permute-start = (f32[8,128]{1,0:T(8,128)S(1)}, f32[8,128]{1,0:T(8,128)S(1)}, u32[]{:S(2)}, u32[]{:S(2)}) collective-permute-start(f32[8,128]{1,0:T(8,128)S(1)} %bitcast.11), channel_id=1, source_target_pairs={{0,1},{1,0},{2,3},{3,2},{4,5},{5,4},{6,7},{7,6},{8,9},{9,8},{10,11... | collective-permute-start | bytes 12296 | tf_op jit(solution)/shard_map/ppermute | solution.py:236
  37.5 3.7 %collective-permute-start.1 = (f32[8,128]{1,0:T(8,128)S(1)}, f32[8,128]{1,0:T(8,128)S(1)}, u32[]{:S(2)}, u32[]{:S(2)}) collective-permute-start(f32[8,128]{1,0:T(8,128)S(1)} %bitcast.12), channel_id=1, source_target_pairs={{0,2},{1,3},{2,0},{3,1},{4,6},{5,7},{6,4},{7,5},{8,10},{9,11},{10,... | collective-permute-start | bytes 12296 | tf_op jit(solution)/shard_map/ppermute | solution.py:236
  39.1 3.0 %copy-start.1 = (f32[128,128]{1,0:T(8,128)}, f32[128,128]{1,0:T(8,128)S(1)}, u32[]{:S(2)}) copy-start(f32[128,128]{1,0:T(8,128)S(1)} %collective-permute-done.3.refs_5_) | copy-start | bytes 196612
  39.1 3.0 %collective-permute-start.2 = (f32[8,128]{1,0:T(8,128)S(1)}, f32[8,128]{1,0:T(8,128)S(1)}, u32[]{:S(2)}, u32[]{:S(2)}) collective-permute-start(f32[8,128]{1,0:T(8,128)S(1)} %bitcast.13), channel_id=1, source_target_pairs={{0,3},{1,2},{2,1},{3,0},{4,7},{5,6},{6,5},{7,4},{8,11},{9,10},{10,... | collective-permute-start | bytes 12296 | tf_op jit(solution)/shard_map/ppermute | solution.py:236
  39.4 2.8 %copy-start.2 = (f32[128,128]{1,0:T(8,128)}, f32[128,128]{1,0:T(8,128)S(1)}, u32[]{:S(2)}) copy-start(f32[128,128]{1,0:T(8,128)S(1)} %collective-permute-done.4.refs_6_) | copy-start | bytes 196612
  39.4 2.8 %copy-start.3 = (f32[128,128]{1,0:T(8,128)}, f32[128,128]{1,0:T(8,128)S(1)}, u32[]{:S(2)}) copy-start(f32[128,128]{1,0:T(8,128)S(1)} %collective-permute-done.5.refs_7_) | copy-start | bytes 196612
  39.4 2.8 %copy-start.5 = (f32[8,128]{1,0:T(8,128)}, f32[8,128]{1,0:T(8,128)S(1)}, u32[]{:S(2)}) copy-start(f32[8,128]{1,0:T(8,128)S(1)} %collective-permute-done.refs_1_) | copy-start | bytes 12292
  41.2 1.0 %copy-start.6 = (f32[8,128]{1,0:T(8,128)}, f32[8,128]{1,0:T(8,128)S(1)}, u32[]{:S(2)}) copy-start(f32[8,128]{1,0:T(8,128)S(1)} %collective-permute-done.1.refs_2_) | copy-start | bytes 12292
  42.1 0.6 %copy-start.7 = (f32[8,128]{1,0:T(8,128)}, f32[8,128]{1,0:T(8,128)S(1)}, u32[]{:S(2)}) copy-start(f32[8,128]{1,0:T(8,128)S(1)} %collective-permute-done.2.refs_3_) | copy-start | bytes 12292

commit v2 on v1

--- a/solution.py
+++ b/solution.py
@@ -17,6 +17,10 @@
 
 VMEM = pl.BlockSpec(memory_space=pltpu.VMEM)
 SMEM = pl.BlockSpec(memory_space=pltpu.SMEM)
+
+
+def held(array):
+    return pltpu.with_memory_space_constraint(array, pltpu.VMEM)
 
 
 def round_up(value, step):
@@ -208,7 +212,7 @@
 
     packed = pl.pallas_call(
         functools.partial(pack_kernel, parts, width),
-        out_shape=jax.ShapeDtypeStruct((parts, rows, LANES), f32),
+        out_shape=pltpu.VMEM((parts, rows, LANES), f32),
         in_specs=[SMEM, SMEM, VMEM, VMEM, VMEM, VMEM],
         out_specs=VMEM,
         scratch_shapes=[pltpu.VMEM((fields, round_up(cells + 2, SUBLANES), length), f32)],
@@ -222,7 +226,7 @@
     me = lax.axis_index("cross").astype(jnp.int32).reshape(1)
     blocks = pl.pallas_call(
         functools.partial(slab_kernel, peers),
-        out_shape=[jax.ShapeDtypeStruct((height, LANES), f32)] * peers,
+        out_shape=[pltpu.VMEM((height, LANES), f32)] * peers,
         in_specs=[SMEM, VMEM, VMEM, VMEM],
         out_specs=[VMEM] * peers,
         cost_estimate=pl.CostEstimate(
@@ -238,10 +242,11 @@
         ]
 
     blocks = exchange(blocks)
+    lines, *blocks = lax.optimization_barrier((lines, *blocks))
 
     moved = pl.pallas_call(
         functools.partial(solve_kernel, parts, fields, cells),
-        out_shape=jax.ShapeDtypeStruct((parts * back, LANES), f32),
+        out_shape=pltpu.VMEM((parts * back, LANES), f32),
         in_specs=[SMEM, SMEM, SMEM, VMEM],
         out_specs=VMEM,
         scratch_shapes=[
@@ -249,7 +254,7 @@
             pltpu.VMEM((fields * parts * cells, LANES), f32),
         ],
         name="solve",
-    )(jacobian, left_vectors, right_vectors, lines)
+    )(jacobian, left_vectors, right_vectors, held(lines))
     moved = lax.all_to_all(moved, "stream", split_axis=0, concat_axis=0, tiled=True)
     squares = moved.reshape(parts, back, LANES)[:, fields * cells, :]
     squares = exchange([squares] * peers)
@@ -264,7 +269,7 @@
         in_specs=[VMEM] * (2 + 2 * peers),
         out_specs=[VMEM, VMEM],
         name="finish",
-    )(adjoint, moved, *squares, *blocks)
+    )(adjoint, *(held(a) for a in (moved, *squares, *blocks)))
     return adjoint_next, sensitivity.reshape(height * LANES)
 
 

time: 44.9 us -> 42.9 us (0.955)
  blocking collectives: 21.9 us -> 10.6 us
  waiting for transfers between devices: 4.95 us -> 12.9 us
  starting transfers between devices: 7.37 us -> 11.1 us
  Pallas kernels: 9.01 us -> 7.4 us
  local copies, waits for them, and re-layouts: 0.58 us -> 0.01 us
    all_to_all x1, blocking collectives: 21.9 us -> 10.6 us  [shards(): lax.all_to_all(moved, 'stream', split_axis=0, concat_axis=0, tiled=True)]
    all_to_all x1, waiting for transfers between devices: 2.21 us -> 6.33 us  [shards(): lax.all_to_all(packed.reshape(parts * rows, LANES), 'stream', split_axis=...]
    ppermute x6, waiting for transfers between devices: 2.74 us -> 6.56 us  [exchange(): lax.ppermute(arrays[k], 'cross', [(i, i ^ k) for i in range(peers)])]
    all_to_all x1, starting transfers between devices: 3.59 us -> 7.28 us  [shards(): lax.all_to_all(packed.reshape(parts * rows, LANES), 'stream', split_axis=...]
    pallas_call x1, Pallas kernels: 1.92 us -> 1.09 us  [shards(): pl.pallas_call(functools.partial(solve_kernel, parts, fields, cells), out...]
    pallas_call x2, Pallas kernels: 5.29 us -> 4.65 us  [the longest x1 2.43 us: shards(): pl.pallas_call(functools.partial(slab_kernel, peers), out_shape=[pltpu.VM...]
    unnamed x16 -> x0, local copies, waits for them, and re-layouts: 0.57 us -> none
  transfers between devices with their start and end apart: 7 -> 7, of which waited for: 3 -> 5; matrix products, arithmetic and copies ran while one was open for 0% -> 0% of each run, Pallas kernels for 7% -> 6%
where the time goes in v2:
time: 42.9 us; the launch traced here: 42.6 us
  waiting for transfers between devices  12.9 us (30%)
  starting transfers between devices  11.1 us (26%)
  blocking collectives  10.6 us (25%)
  Pallas kernels  7.4 us (17%)
  between operations  0.66 us (2%)
    all_to_all x1, blocking collectives, shards(): lax.all_to_all(moved, 'stream', split_axis=0, concat_axis=0, tiled=True)  10.6 us
    all_to_all x1, starting transfers between devices, shards(): lax.all_to_all(packed.reshape(parts * rows, LANES), 'stream', split_axis=...  7.28 us
    ppermute x6, waiting for transfers between devices, exchange(): lax.ppermute(arrays[k], 'cross', [(i, i ^ k) for i in range(peers)])  6.56 us
    all_to_all x1, waiting for transfers between devices, shards(): lax.all_to_all(packed.reshape(parts * rows, LANES), 'stream', split_axis=...  6.33 us
    ppermute x6, starting transfers between devices, exchange(): lax.ppermute(arrays[k], 'cross', [(i, i ^ k) for i in range(peers)])  3.77 us
    pallas_call x1, Pallas kernels, shards(): pl.pallas_call(functools.partial(slab_kernel, peers), out_shape=[pltpu.VM...  2.43 us
    pallas_call x1, Pallas kernels, shards(): pl.pallas_call(functools.partial(pack_kernel, parts, width), out_shape=pl...  2.23 us
    pallas_call x1, Pallas kernels, shards(): pl.pallas_call(functools.partial(finish_kernel, parts, width, peers, cell...  1.65 us
  transfers between devices with their start and end apart: 7, of which 5 were waited for; matrix products, arithmetic and copies ran while one was open for 0% of the time, Pallas kernels for 6%

profile of v2, /device:TPU:0, one launch (start us, length us, event | category | flops | bytes accessed | tf_op | source)
XLA Modules:
  0.0 42.6 jit_solution(10551672719255656868)
XLA Ops:
  0.6 2.2 %pack.1 = f32[8,128,128]{2,1,0:T(8,128)} custom-call(f32[5,5]{1,0:T(8,128)} %jac.3, f32[5,5]{1,0:T(8,128)} %left.3, f32[5,4,1024]{2,1,0:T(4,128)} %adj.5, f32[5,4,1024]{2,1,0:T(4,128)} %src.1, f32[2,5,4,1024]{3,2,1,0:T(4,128)} %low.1, f32[3,5,4,1024]{3,2,1,0:T(4,128)} %up.1), custom_call_target="tpu_custom_call" | custom-call | tf_op jit(solution)/shard_map/pack/pallas_call | solution.py:213
  2.9 7.3 %all-to-all-start = ((f32[8,128,128]{2,1,0:T(8,128)}), f32[8,128,128]{2,1,0:T(8,128)S(1)}, u32[]{:S(2)}, u32[]{:S(2)}) async-start(f32[8,128,128]{2,1,0:T(8,128)} %pack.1), calls=%async_computation | async-start | bytes 1048576 | tf_op jit(solution)/shard_map/all_to_all | solution.py:221
  10.1 2.4 %slab.1 = (f32[128,128]{1,0:T(8,128)S(1)}, f32[128,128]{1,0:T(8,128)S(1)}, f32[128,128]{1,0:T(8,128)S(1)}, f32[128,128]{1,0:T(8,128)S(1)}) custom-call(s32[1]{0:T(128)} %bitcast.1.me, f32[5,4,1024]{2,1,0:T(4,128)} %adj.5, f32[5,4,1024]{2,1,0:T(4,128)} %grad.1, s32[4,1024]{1,0:T(4,128)} %ctrl.1), custom_call_target="tpu_custom_call" | custom-call | flops 1073741824 | bytes 4194304 | tf_op jit(solution)/shard_map/slab/pallas_call | solution.py:227
  12.6 0.1 collective-permute-start
  12.7 1.6 %collective-permute-start.1 = (f32[128,128]{1,0:T(8,128)S(1)}, f32[128,128]{1,0:T(8,128)S(1)}, u32[]{:S(2)}, u32[]{:S(2)}) collective-permute-start(f32[128,128]{1,0:T(8,128)S(1)} %get-tuple-element.15), channel_id=1, source_target_pairs={{0,2},{1,3},{2,0},{3,1},{4,6},{5,7},{6,4},{7,5},{8,10},{9,11},{10,... | collective-permute-start | bytes 196616 | tf_op jit(solution)/shard_map/ppermute | solution.py:240
  14.2 0.3 collective-permute-start.2
  14.5 0.0 collective-permute-done.refs_5_
  14.5 2.6 %collective-permute-done.1.refs_6_ = f32[128,128]{1,0:T(8,128)S(1)} collective-permute-done((f32[128,128]{1,0:T(8,128)S(1)}, f32[128,128]{1,0:T(8,128)S(1)}, u32[]{:S(2)}, u32[]{:S(2)}) %collective-permute-start.1) | collective-permute-done | bytes 65568 | tf_op jit(solution)/shard_map/ppermute | solution.py:240
  17.1 1.2 %collective-permute-done.2.refs_7_ = f32[128,128]{1,0:T(8,128)S(1)} collective-permute-done((f32[128,128]{1,0:T(8,128)S(1)}, f32[128,128]{1,0:T(8,128)S(1)}, u32[]{:S(2)}, u32[]{:S(2)}) %collective-permute-start.2) | collective-permute-done | bytes 65568 | tf_op jit(solution)/shard_map/ppermute | solution.py:240
  18.3 6.3 %all-to-all-done = f32[8,128,128]{2,1,0:T(8,128)S(1)} async-done(((f32[8,128,128]{2,1,0:T(8,128)}), f32[8,128,128]{2,1,0:T(8,128)S(1)}, u32[]{:S(2)}, u32[]{:S(2)}) %all-to-all-start) | async-done | bytes 524320 | tf_op jit(solution)/shard_map/all_to_all | solution.py:221
  24.6 1.1 %solve.1 = f32[192,128]{1,0:T(8,128)S(1)} custom-call(f32[5,5]{1,0:T(8,128)} %jac.3, f32[5,5]{1,0:T(8,128)} %left.3, f32[5,5]{1,0:T(8,128)} %right.1, f32[1024,128]{1,0:T(8,128)S(1)} %bitcast.8), custom_call_target="tpu_custom_call" | custom-call | tf_op jit(solution)/shard_map/solve/pallas_call | solution.py:247
  25.7 10.6 %all_to_all.20 = f32[8,24,128]{2,1,0:T(8,128)S(1)} all-to-all(f32[8,24,128]{2,1,0:T(8,128)S(1)} %bitcast.10), channel_id=1, replica_groups=mesh['stream'=8,'cross'=4] {'stream'}, dimensions={0} | all-to-all | bytes 196608 | tf_op jit(solution)/shard_map/all_to_all | solution.py:258
  36.3 0.0 collective-permute-start.3
  36.3 1.6 %collective-permute-start.4 = (f32[8,128]{1,0:T(8,128)S(1)}, f32[8,128]{1,0:T(8,128)S(1)}, u32[]{:S(2)}, u32[]{:S(2)}) collective-permute-start(f32[8,128]{1,0:T(8,128)S(1)} %bitcast.12), channel_id=1, source_target_pairs={{0,2},{1,3},{2,0},{3,1},{4,6},{5,7},{6,4},{7,5},{8,10},{9,11},{10,... | collective-permute-start | bytes 12296 | tf_op jit(solution)/shard_map/ppermute | solution.py:240
  37.9 0.3 collective-permute-start.5
  38.1 0.0 collective-permute-done.3.refs_1_
  38.1 1.8 %collective-permute-done.4.refs_2_ = f32[8,128]{1,0:T(8,128)S(1)} collective-permute-done((f32[8,128]{1,0:T(8,128)S(1)}, f32[8,128]{1,0:T(8,128)S(1)}, u32[]{:S(2)}, u32[]{:S(2)}) %collective-permute-start.4) | collective-permute-done | bytes 4128 | tf_op jit(solution)/shard_map/ppermute | solution.py:240
  40.0 0.9 %collective-permute-done.5.refs_3_ = f32[8,128]{1,0:T(8,128)S(1)} collective-permute-done((f32[8,128]{1,0:T(8,128)S(1)}, f32[8,128]{1,0:T(8,128)S(1)}, u32[]{:S(2)}, u32[]{:S(2)}) %collective-permute-start.5) | collective-permute-done | bytes 4128 | tf_op jit(solution)/shard_map/ppermute | solution.py:240
  40.9 1.6 %finish.1 = (f32[5,4,1024]{2,1,0:T(4,128)}, f32[128,128]{1,0:T(8,128)}) custom-call(f32[5,4,1024]{2,1,0:T(4,128)} %adj.5, f32[192,128]{1,0:T(8,128)S(1)} %bitcast.9, f32[8,128]{1,0:T(8,128)S(1)} %bitcast.14, f32[8,128]{1,0:T(8,128)S(1)} %collective-permute-done.3.refs_1_, f32[8,128]{1,0:T(8,128)S(1)} %collective-permute-done.4.refs_2_, ...), custom_call_target="tpu_custom_call" | custom-call | tf_op jit(solution)/shard_map/finish/pallas_call | solution.py:263
  (1 shorter events, 0.0 us)
Async XLA Ops:
  2.9 21.8 %all-to-all-start = ((f32[8,128,128]{2,1,0:T(8,128)}), f32[8,128,128]{2,1,0:T(8,128)S(1)}, u32[]{:S(2)}, u32[]{:S(2)}) async-start(f32[8,128,128]{2,1,0:T(8,128)} %pack.1), calls=%async_computation | async-start | bytes 1048576 | tf_op jit(solution)/shard_map/all_to_all | solution.py:221
  12.6 1.9 %collective-permute-start = (f32[128,128]{1,0:T(8,128)S(1)}, f32[128,128]{1,0:T(8,128)S(1)}, u32[]{:S(2)}, u32[]{:S(2)}) collective-permute-start(f32[128,128]{1,0:T(8,128)S(1)} %get-tuple-element.14), channel_id=1, source_target_pairs={{0,1},{1,0},{2,3},{3,2},{4,5},{5,4},{6,7},{7,6},{8,9},{9,8},{10,11... | collective-permute-start | bytes 196616 | tf_op jit(solution)/shard_map/ppermute | solution.py:240
  12.7 4.5 %collective-permute-start.1 = (f32[128,128]{1,0:T(8,128)S(1)}, f32[128,128]{1,0:T(8,128)S(1)}, u32[]{:S(2)}, u32[]{:S(2)}) collective-permute-start(f32[128,128]{1,0:T(8,128)S(1)} %get-tuple-element.15), channel_id=1, source_target_pairs={{0,2},{1,3},{2,0},{3,1},{4,6},{5,7},{6,4},{7,5},{8,10},{9,11},{10,... | collective-permute-start | bytes 196616 | tf_op jit(solution)/shard_map/ppermute | solution.py:240
  14.2 4.1 %collective-permute-start.2 = (f32[128,128]{1,0:T(8,128)S(1)}, f32[128,128]{1,0:T(8,128)S(1)}, u32[]{:S(2)}, u32[]{:S(2)}) collective-permute-start(f32[128,128]{1,0:T(8,128)S(1)} %get-tuple-element.16), channel_id=1, source_target_pairs={{0,3},{1,2},{2,1},{3,0},{4,7},{5,6},{6,5},{7,4},{8,11},{9,10},{10,... | collective-permute-start | bytes 196616 | tf_op jit(solution)/shard_map/ppermute | solution.py:240
  36.3 1.9 %collective-permute-start.3 = (f32[8,128]{1,0:T(8,128)S(1)}, f32[8,128]{1,0:T(8,128)S(1)}, u32[]{:S(2)}, u32[]{:S(2)}) collective-permute-start(f32[8,128]{1,0:T(8,128)S(1)} %bitcast.11), channel_id=1, source_target_pairs={{0,1},{1,0},{2,3},{3,2},{4,5},{5,4},{6,7},{7,6},{8,9},{9,8},{10,11... | collective-permute-start | bytes 12296 | tf_op jit(solution)/shard_map/ppermute | solution.py:240
  36.3 3.7 %collective-permute-start.4 = (f32[8,128]{1,0:T(8,128)S(1)}, f32[8,128]{1,0:T(8,128)S(1)}, u32[]{:S(2)}, u32[]{:S(2)}) collective-permute-start(f32[8,128]{1,0:T(8,128)S(1)} %bitcast.12), channel_id=1, source_target_pairs={{0,2},{1,3},{2,0},{3,1},{4,6},{5,7},{6,4},{7,5},{8,10},{9,11},{10,... | collective-permute-start | bytes 12296 | tf_op jit(solution)/shard_map/ppermute | solution.py:240
  37.9 3.0 %collective-permute-start.5 = (f32[8,128]{1,0:T(8,128)S(1)}, f32[8,128]{1,0:T(8,128)S(1)}, u32[]{:S(2)}, u32[]{:S(2)}) collective-permute-start(f32[8,128]{1,0:T(8,128)S(1)} %bitcast.13), channel_id=1, source_target_pairs={{0,3},{1,2},{2,1},{3,0},{4,7},{5,6},{6,5},{7,4},{8,11},{9,10},{10,... | collective-permute-start | bytes 12296 | tf_op jit(solution)/shard_map/ppermute | solution.py:240

commit v3 on v2

v3 whole, which is shorter than its diff:
```python
import functools

import jax
import jax.numpy as jnp
from jax import lax
from jax.experimental import pallas as pl
from jax.experimental.pallas import tpu as pltpu
from jax.sharding import PartitionSpec as P

NCTRL = 524288
LANES = 128
SUBLANES = 8

dissipation = 0.25
step_scale = 0.5
epsilon = 1e-06

VMEM = pl.BlockSpec(memory_space=pltpu.VMEM)
SMEM = pl.BlockSpec(memory_space=pltpu.SMEM)


def held(array):
    return pltpu.with_memory_space_constraint(array, pltpu.VMEM)


def round_up(value, step):
    return -(-value // step) * step


def mix(matrix_ref, columns):
    count = len(columns)
    return [
        sum(matrix_ref[f, g] * columns[g] for g in range(1, count)) + matrix_ref[f, 0] * columns[0]
        for f in range(count)
    ]


CELL_KINDS = 5


def block_rows(fields, cells):
    return round_up(fields * (CELL_KINDS * cells + cells - 1 + 2), SUBLANES)


def spread(scratch, me, outs):
    for k, out in enumerate(outs):
        out[...] = scratch[lax.bitwise_xor(me[0], k)]


def pack_kernel(group, width, me, jac, left, adj, src, low, up, *refs):
    outs, (blocks, pad) = refs[:group], refs[group:]
    fields, cells, length = adj.shape
    rows = block_rows(fields, cells)
    if width < LANES or rows > fields * (CELL_KINDS * cells + cells + 1):
        blocks[...] = jnp.zeros_like(blocks)
    pad[...] = jnp.zeros_like(pad)
    for f in range(fields):
        pad[f, 1 : cells + 1, :] = adj[f]
    ahead = [pad[f, 2 : cells + 2, :] for f in range(fields)]
    behind = [pad[f, 0:cells, :] for f in range(fields)]
    central = mix(jac, [a - b for a, b in zip(ahead, behind)])
    residual = [
        src[f] - 0.5 * central[f] + dissipation * (ahead[f] - 2.0 * adj[f] + behind[f])
        for f in range(fields)
    ]
    characteristic = mix(left, residual)
    cell = lax.broadcasted_iota(jnp.int32, (cells, length), 0)
    extra = CELL_KINDS * fields * cells
    for f in range(fields):
        diagonal = up[0, f]
        inverse = 1.0 / diagonal
        own = jnp.where(cell == 1, inverse, 1.0)
        diagonal_1 = jnp.broadcast_to(up[0, f, 1:2, :], (cells, length))
        values = (
            characteristic[f] * own,
            low[0, f] * jnp.where(cell == 2, diagonal_1, own),
            low[1, f] * jnp.where(cell == 3, diagonal_1, own),
            up[1, f] * inverse,
            up[2, f] * inverse,
        )
        for d, base, lanes, to in pieces(group, width, rows):
            for k, value in enumerate(values):
                at = base + (k * fields + f) * cells
                blocks[d, at : at + cells, to] = value[:, lanes]
            at = base + extra + f * (cells + 1)
            blocks[d, at : at + 1, to] = inverse[0:1, lanes]
            blocks[d, at + 1 : at + cells - 1, to] = inverse[2:cells, lanes]
            blocks[d, at + cells - 1 : at + cells, to] = adj[f, 0:1, lanes]
            blocks[d, at + cells : at + cells + 1, to] = adj[f, cells - 1 : cells, lanes]
    spread(blocks, me, outs)


def pieces(group, width, rows):
    step = min(width, LANES)
    for d in range(group):
        for b in range(width // step):
            start = d * width + b * step
            yield d, b * rows, slice(start, start + step), slice(0, step)


class Lines:
    def __init__(self, ref, fields, cells, base):
        self.ref, self.fields, self.cells, self.base = ref, fields, cells, base

    def value(self, d, k, i):
        at = self.base(d) + k * self.fields * self.cells + i
        return self.ref[pl.ds(at, self.fields, stride=self.cells), :]

    def divided(self, d, i, value):
        if i == 1:
            return value
        at = self.base(d) + CELL_KINDS * self.fields * self.cells + (i if i == 0 else i - 1)
        return value * self.ref[pl.ds(at, self.fields, stride=self.cells + 1), :]


def less(value, factor, other):
    if other is None:
        return value
    return -(factor * other) if value is None else value - factor * other


SLOTS = 8


def sweep_kernel(group, fields, cells, me, half, jac, left, *refs):
    received, (lines, edge, message) = refs[:group], refs[group:]
    rows = block_rows(fields, cells)
    size = received[0].shape[0]
    count = size // rows
    for k in range(group):
        at = pl.multiple_of(lax.bitwise_xor(me[0], k) * size, SUBLANES)
        lines[pl.ds(at, size), :] = received[k][...]
    lower_half = jnp.full((fields, LANES), half[0], jnp.int32) == 0
    extra = CELL_KINDS * fields * cells
    for b in range(count):

        def across(row):
            return lines[pl.ds(b * rows + row, group, stride=size), :]

        firsts = [across(extra + f * (cells + 1) + cells - 1) for f in range(fields)]
        lasts = [across(extra + f * (cells + 1) + cells) for f in range(fields)]
        from_last = mix(jac, lasts)
        from_first = mix(jac, firsts)
        into_first = mix(left, [0.5 * x + dissipation * y for x, y in zip(from_last, lasts)])
        into_last = mix(left, [dissipation * y - 0.5 * x for x, y in zip(from_first, firsts)])
        at = 2 * b * fields * group
        for f in range(fields):
            edge[at + f * group : at + (f + 1) * group, :] = into_first[f]
            edge[at + (fields + f) * group : at + (fields + f + 1) * group, :] = into_last[f]

        def to_next(d):
            return edge[pl.ds(at + d, fields, stride=group), :]

        def to_previous(d):
            return edge[pl.ds(at + fields * group + d, fields, stride=group), :]

        view = Lines(lines, fields, cells, lambda d: (d * count + b) * rows)
        ones = jnp.ones((fields, LANES), jnp.float32)
        one, two = [None, ones, None], [None, None, None]
        forward = {}
        for d in range(group):
            for i in range(cells):
                value = view.value(d, 0, i)
                if i == 0 and d > 0:
                    value = value + to_next(d - 1)
                if i == cells - 1 and d < group - 1:
                    value = value + to_previous(d + 1)
                start = [value, None, ones if d == 0 and i == 0 else None]
                first, second = view.value(d, 1, i), view.value(d, 2, i)
                now = [less(less(start[c], second, two[c]), first, one[c]) for c in range(3)]
                forward[d, i] = now
                one, two = now, one
        ends = [one[0], two[0], to_next(group - 1)]
        one, two = [None] * 3, [None] * 3
        for d in reversed(range(group)):
            for i in reversed(range(cells)):
                start = [view.divided(d, i, value) for value in forward[d, i]]
                first, second = view.value(d, 3, i), view.value(d, 4, i)
                now = [less(less(start[c], second, two[c]), first, one[c]) for c in range(3)]
                one, two = now, one
        begins = [one[0], two[0], to_previous(0)]
        slots = [jnp.where(lower_half, x, y) for x, y in zip(ends, begins)]
        slots += [one[1], two[1], one[2], two[2], view.value(0, 2, 0)]
        for k, value in enumerate(slots):
            row = (b * SLOTS + k) * fields
            message[row : row + fields, :] = value


def solve_kernel(group, fields, cells, me, half, right, lines, edge, mine, other, *refs):
    outs, (squares, whole, blocks) = refs[:group], refs[group:]
    rows = block_rows(fields, cells)
    size = lines.shape[0] // group
    count = size // rows
    total = group * cells
    lower_half = jnp.full((fields, LANES), half[0], jnp.int32) == 0
    summed = None
    for b in range(count):
        view = Lines(lines, fields, cells, lambda d: (d * count + b) * rows)
        at = 2 * b * fields * group

        def to_next(d):
            return edge[pl.ds(at + d, fields, stride=group), :]

        def to_previous(d):
            return edge[pl.ds(at + fields * group + d, fields, stride=group), :]

        def slot(ref, k):
            row = (b * SLOTS + k) * fields
            return ref[row : row + fields, :]

        def of_lower(k):
            return jnp.where(lower_half, slot(mine, k), slot(other, k))

        def of_upper(k):
            return jnp.where(lower_half, slot(other, k), slot(mine, k))

        zeros = jnp.zeros((fields, LANES), jnp.float32)
        onto_last, onto_first = of_upper(2), of_lower(2)
        before, before_2 = of_lower(0) + onto_last, of_lower(1)
        added = onto_first - of_upper(7) * before_2
        after = of_upper(0) + of_upper(3) * before + of_upper(5) * added
        after_2 = of_upper(1) + of_upper(4) * before + of_upper(6) * added
        one, two = jnp.where(lower_half, zeros, before), jnp.where(lower_half, zeros, before_2)
        onto_first = jnp.where(lower_half, zeros, onto_first)
        onto_last = jnp.where(lower_half, onto_last, zeros)
        forward = {}
        for d in range(group):
            for i in range(cells):
                value = view.value(d, 0, i)
                if i == 0:
                    value = value + (to_next(d - 1) if d > 0 else onto_first)
                if i == cells - 1:
                    value = value + (to_previous(d + 1) if d < group - 1 else onto_last)
                value = less(less(value, view.value(d, 2, i), two), view.value(d, 1, i), one)
                forward[d, i] = value
                one, two = value, one
        one, two = jnp.where(lower_half, after, zeros), jnp.where(lower_half, after_2, zeros)
        for d in reversed(range(group)):
            for i in reversed(range(cells)):
                value = view.divided(d, i, forward[d, i])
                value = less(less(value, view.value(d, 4, i), two), view.value(d, 3, i), one)
                whole[pl.ds(b * fields * total + d * cells + i, fields, stride=total), :] = value
                one, two = value, one
        columns = [(b * fields + g) * total for g in range(fields)]
        increment = mix(right, [whole[at : at + total, :] for at in columns])
        for f in range(fields):
            part = jnp.sum(increment[f] * increment[f], axis=0, keepdims=True)
            summed = part if summed is None else summed + part
            for d in range(group):
                row = (b * fields + f) * cells
                blocks[d, row : row + cells, :] = increment[f][d * cells : (d + 1) * cells, :]
    spread(blocks, me, outs)
    for n in range(squares.shape[0]):
        squares[n] = summed


def slab_kernel(peers, me, adj, grad, ctrl, *outs):
    fields, cells, length = adj.shape
    height = outs[0].shape[0]
    contribution = adj[0] * grad[0]
    for f in range(1, fields):
        contribution = contribution + adj[f] * grad[f]
    upper = contribution.astype(jnp.bfloat16).astype(jnp.float32)
    lower = contribution - upper
    high = lax.shift_right_logical(ctrl[...], 7)
    low = lax.bitwise_and(ctrl[...], LANES - 1)
    block = lax.broadcasted_iota(jnp.int32, (height, length), 0)
    lane = lax.broadcasted_iota(jnp.int32, (LANES, length), 0)
    sums = None
    for i in range(cells):
        hit = lane == low[i : i + 1, :]
        terms = jnp.concatenate(
            [
                jnp.where(hit, upper[i : i + 1, :], 0.0).astype(jnp.bfloat16),
                jnp.where(hit, lower[i : i + 1, :], 0.0).astype(jnp.bfloat16),
            ],
            axis=0,
        )
        rows = []
        for k in range(peers):
            offset = lax.bitwise_xor(me[0], k) * height
            rows.append(jnp.where(block == high[i : i + 1, :] - offset, 1.0, 0.0).astype(jnp.bfloat16))
        picked = jnp.concatenate(rows, axis=0)
        part = lax.dot_general(
            picked, terms, (((1,), (1,)), ((), ())), preferred_element_type=jnp.float32
        )
        sums = part if sums is None else sums + part
    sums = sums[:, :LANES] + sums[:, LANES:]
    for k in range(peers):
        outs[k][...] = sums[k * height : (k + 1) * height, :]


def finish_kernel(group, width, peers, cell_count, me, adj, squares, *refs):
    moved, slabs, (out, sens, blocks) = refs[:group], refs[group : group + peers], refs[group + peers :]
    fields, cells, _ = adj.shape
    for k in range(group):
        blocks[lax.bitwise_xor(me[0], k)] = moved[k][...]
    slab = slabs[0][...]
    for k in range(1, peers):
        slab = slab + slabs[k][...]
    sens[...] = slab
    total = jnp.sum(jnp.sum(squares[...], axis=0), axis=1, keepdims=True)
    factor = step_scale / jnp.sqrt(total / cell_count + epsilon)
    for d, base, lanes, to in pieces(group, width, fields * cells):
        for f in range(fields):
            at = base + f * cells
            out[f, :, lanes] = adj[f, :, lanes] + factor * blocks[d, at : at + cells, to]


def swap(array, axis, k):
    return lax.ppermute(array, axis, [(i, i ^ k) for i in range(lax.axis_size(axis))])


def exchange(arrays, axis):
    return [arrays[0]] + [swap(arrays[k], axis, k) for k in range(1, len(arrays))]


def shards(
    adjoint, source, shape_grad, lower_band, upper_band, jacobian, left_vectors, right_vectors, ctrl_local
):
    fields, cells, length = adjoint.shape
    parts, peers = lax.axis_size("stream"), lax.axis_size("cross")
    group = parts // 2
    width = length // group
    count = -(-width // LANES)
    rows = count * block_rows(fields, cells)
    back = count * fields * cells
    f32 = jnp.float32

    at = lax.axis_index("stream").astype(jnp.int32)
    me, half = (at % group).reshape(1), (at // group).reshape(1)
    packed = pl.pallas_call(
        functools.partial(pack_kernel, group, width),
        out_shape=[pltpu.VMEM((rows, LANES), f32)] * group,
        in_specs=[SMEM, SMEM, SMEM, VMEM, VMEM, VMEM, VMEM],
        out_specs=[VMEM] * group,
        scratch_shapes=[
            pltpu.VMEM((group, rows, LANES), f32),
            pltpu.VMEM((fields, round_up(cells + 2, SUBLANES), length), f32),
        ],
        name="pack",
    )(me, jacobian, left_vectors, adjoint, source, lower_band, upper_band)
    received = exchange(packed, "stream")

    height = NCTRL // (parts * peers * LANES)
    column = lax.axis_index("cross").astype(jnp.int32).reshape(1)
    slabs = pl.pallas_call(
        functools.partial(slab_kernel, peers),
        out_shape=[pltpu.VMEM((height, LANES), f32)] * peers,
        in_specs=[SMEM, VMEM, VMEM, VMEM],
        out_specs=[VMEM] * peers,
        cost_estimate=pl.CostEstimate(
            flops=4 * cells * length * NCTRL // parts, bytes_accessed=4 << 20, transcendentals=0
        ),
        name="slab",
    )(column, adjoint, shape_grad, ctrl_local)
    *received, slabs = lax.optimization_barrier((*received, slabs))

    lines, edge, message = pl.pallas_call(
        functools.partial(sweep_kernel, group, fields, cells),
        out_shape=[
            pltpu.VMEM((group * rows, LANES), f32),
            pltpu.VMEM((2 * count * fields * group, LANES), f32),
            pltpu.VMEM((count * SLOTS * fields, LANES), f32),
        ],
        in_specs=[SMEM] * 4 + [VMEM] * group,
        out_specs=[VMEM] * 3,
        name="sweep",
    )(me, half, jacobian, left_vectors, *(held(a) for a in received))
    other = swap(message, "stream", group)
    slabs = exchange(slabs, "cross")
    other, *slabs = lax.optimization_barrier((other, *slabs))

    *moved, squares = pl.pallas_call(
        functools.partial(solve_kernel, group, fields, cells),
        out_shape=[pltpu.VMEM((back, LANES), f32)] * group
        + [pltpu.VMEM((parts * peers, 1, LANES), f32)],
        in_specs=[SMEM] * 3 + [VMEM] * 4,
        out_specs=[VMEM] * (group + 1),
        scratch_shapes=[
            pltpu.VMEM((count * fields * group * cells, LANES), f32),
            pltpu.VMEM((group, back, LANES), f32),
        ],
        name="solve",
    )(me, half, right_vectors, *(held(a) for a in (lines, edge, message, other)))
    squares = lax.all_to_all(squares, ("stream", "cross"), split_axis=0, concat_axis=0, tiled=True)
    moved = exchange(moved, "stream")

    cell_count = fields * cells * length * parts * peers
    adjoint_next, sensitivity = pl.pallas_call(
        functools.partial(finish_kernel, group, width, peers, cell_count),
        out_shape=[
            jax.ShapeDtypeStruct(adjoint.shape, f32),
            jax.ShapeDtypeStruct((height, LANES), f32),
        ],
        in_specs=[SMEM] + [VMEM] * (2 + group + peers),
        out_specs=[VMEM, VMEM],
        scratch_shapes=[pltpu.VMEM((group, back, LANES), f32)],
        name="finish",
    )(me, adjoint, *(held(a) for a in (squares, *moved, *slabs)))
    return adjoint_next, sensitivity.reshape(height * LANES)


def solution(mesh):
    in_specs = (
        P(None, "stream", "cross"),
        P(None, "stream", "cross"),
        P(None, "stream", "cross"),
        P(None, None, "stream", "cross"),
        P(None, None, "stream", "cross"),
        P(),
        P(),
        P(),
        P("stream", "cross"),
    )
    out_specs = (P(None, "stream", "cross"), P(("stream", "cross")))
    return jax.shard_map(shards, mesh=mesh, in_specs=in_specs, out_specs=out_specs, check_vma=False)
```

time: 42.9 us -> 38.6 us (0.90)
  blocking collectives: 10.6 us -> 0 us
  starting transfers between devices: 11.1 us -> 19.4 us
  waiting for transfers between devices: 12.9 us -> 10.1 us
  Pallas kernels: 7.4 us -> 8.11 us
    all_to_all x1 -> x0, blocking collectives: 10.6 us -> none  [shards(): lax.all_to_all(moved, 'stream', split_axis=0, concat_axis=0, tiled=True)]
    ppermute x6 -> x10, starting transfers between devices: 3.77 us -> 12.9 us  [swap(): lax.ppermute(array, axis, [(i, i ^ k) for i in range(lax.axis_size(axis))])]
    all_to_all x1, waiting for transfers between devices: 6.33 us -> 0.01 us  [shards(): lax.all_to_all(squares, ('stream', 'cross'), split_axis=0, concat_axis=0,...]
    ppermute x6 -> x10, waiting for transfers between devices: 6.56 us -> 10.1 us  [swap(): lax.ppermute(array, axis, [(i, i ^ k) for i in range(lax.axis_size(axis))])]
    all_to_all x1, starting transfers between devices: 7.28 us -> 6.53 us  [shards(): lax.all_to_all(squares, ('stream', 'cross'), split_axis=0, concat_axis=0,...]
    pallas_call x3 -> x4, Pallas kernels: 4.97 us -> 5.68 us  [the longest x1 1.68 us: shards(): pl.pallas_call(functools.partial(finish_kernel, group, width, peers, cell...]
  transfers between devices with their start and end apart: 7 -> 11, of which waited for: 5 -> 6; matrix products, arithmetic and copies ran while one was open for 0% -> 0% of each run, Pallas kernels for 6% -> 9%
where the time goes in v3:
time: 38.6 us; the launch traced here: 38.3 us
  starting transfers between devices  19.4 us (50%)
  waiting for transfers between devices  10.1 us (26%)
  Pallas kernels  8.11 us (21%)
  between operations  0.69 us (2%)
    ppermute x10, starting transfers between devices, swap(): lax.ppermute(array, axis, [(i, i ^ k) for i in range(lax.axis_size(axis))])  12.9 us
    ppermute x10, waiting for transfers between devices, swap(): lax.ppermute(array, axis, [(i, i ^ k) for i in range(lax.axis_size(axis))])  10.1 us
    all_to_all x1, starting transfers between devices, shards(): lax.all_to_all(squares, ('stream', 'cross'), split_axis=0, concat_axis=0,...  6.53 us
    pallas_call x1, Pallas kernels, shards(): pl.pallas_call(functools.partial(slab_kernel, peers), out_shape=[pltpu.VM...  2.43 us
    pallas_call x1, Pallas kernels, shards(): pl.pallas_call(functools.partial(finish_kernel, group, width, peers, cell...  1.68 us
    pallas_call x1, Pallas kernels, shards(): pl.pallas_call(functools.partial(solve_kernel, group, fields, cells), out...  1.5 us
    pallas_call x1, Pallas kernels, shards(): pl.pallas_call(functools.partial(pack_kernel, group, width), out_shape=[p...  1.47 us
    pallas_call x1, Pallas kernels, shards(): pl.pallas_call(functools.partial(sweep_kernel, group, fields, cells), out...  1.04 us
  transfers between devices with their start and end apart: 11, of which 6 were waited for; matrix products, arithmetic and copies ran while one was open for 0% of the time, Pallas kernels for 9%

profile of v3, /device:TPU:0, one launch (start us, length us, event | category | flops | bytes accessed | tf_op | source)
XLA Modules:
  0.0 38.3 jit_solution(9505219012688504436)
XLA Ops:
  0.6 1.5 %pack.1 = (f32[256,128]{1,0:T(8,128)S(1)}, f32[256,128]{1,0:T(8,128)S(1)}, f32[256,128]{1,0:T(8,128)S(1)}, f32[256,128]{1,0:T(8,128)S(1)}) custom-call(s32[1]{0:T(128)} %bitcast.me, f32[5,5]{1,0:T(8,128)} %jac.3, f32[5,5]{1,0:T(8,128)} %left.3, f32[5,4,1024]{2,1,0:T(4,128)} %adj.5, f32[5,4,1024]{2,1,0:T(4,128)} %src.1, f32[2,5,4,1024]{3,2,1,0:T(4,128)} %low.1, ...), custom_call_target="tpu_custom_call" | custom-call | tf_op jit(solution)/shard_map/pack/pallas_call | solution.py:332
  2.1 3.0 %collective-permute-start = (f32[256,128]{1,0:T(8,128)S(1)}, f32[256,128]{1,0:T(8,128)S(1)}, u32[]{:S(2)}, u32[]{:S(2)}) collective-permute-start(f32[256,128]{1,0:T(8,128)S(1)} %get-tuple-element.34), channel_id=1, source_target_pairs={{0,4},{4,0},{8,12},{12,8},{16,20},{20,16},{24,28},{28,24},{1,5},{5... | collective-permute-start | bytes 393224 | tf_op jit(solution)/shard_map/ppermute | solution.py:311
  5.2 1.6 %collective-permute-start.1 = (f32[256,128]{1,0:T(8,128)S(1)}, f32[256,128]{1,0:T(8,128)S(1)}, u32[]{:S(2)}, u32[]{:S(2)}) collective-permute-start(f32[256,128]{1,0:T(8,128)S(1)} %get-tuple-element.35), channel_id=1, source_target_pairs={{0,8},{4,12},{8,0},{12,4},{16,24},{20,28},{24,16},{28,20},{1,9},{5... | collective-permute-start | bytes 393224 | tf_op jit(solution)/shard_map/ppermute | solution.py:311
  6.7 0.0 collective-permute-start.2
  6.7 2.4 %slab.1 = (f32[128,128]{1,0:T(8,128)S(1)}, f32[128,128]{1,0:T(8,128)S(1)}, f32[128,128]{1,0:T(8,128)S(1)}, f32[128,128]{1,0:T(8,128)S(1)}) custom-call(s32[1]{0:T(128)} %bitcast.2.me, f32[5,4,1024]{2,1,0:T(4,128)} %adj.5, f32[5,4,1024]{2,1,0:T(4,128)} %grad.1, s32[4,1024]{1,0:T(4,128)} %ctrl.1), custom_call_target="tpu_custom_call" | custom-call | flops 1073741824 | bytes 4194304 | tf_op jit(solution)/shard_map/slab/pallas_call | solution.py:347
  9.2 0.0 collective-permute-done.refs_1_
  9.2 2.3 %collective-permute-done.1.refs_2_ = f32[256,128]{1,0:T(8,128)S(1)} collective-permute-done((f32[256,128]{1,0:T(8,128)S(1)}, f32[256,128]{1,0:T(8,128)S(1)}, u32[]{:S(2)}, u32[]{:S(2)}) %collective-permute-start.1) | collective-permute-done | bytes 131104 | tf_op jit(solution)/shard_map/ppermute | solution.py:311
  11.5 1.2 %collective-permute-done.2.refs_3_ = f32[256,128]{1,0:T(8,128)S(1)} collective-permute-done((f32[256,128]{1,0:T(8,128)S(1)}, f32[256,128]{1,0:T(8,128)S(1)}, u32[]{:S(2)}, u32[]{:S(2)}) %collective-permute-start.2) | collective-permute-done | bytes 131104 | tf_op jit(solution)/shard_map/ppermute | solution.py:311
  12.7 0.0 collective-permute-start.4
  12.7 1.7 %collective-permute-start.5 = (f32[128,128]{1,0:T(8,128)S(1)}, f32[128,128]{1,0:T(8,128)S(1)}, u32[]{:S(2)}, u32[]{:S(2)}) collective-permute-start(f32[128,128]{1,0:T(8,128)S(1)} %get-tuple-element.50), channel_id=1, source_target_pairs={{0,2},{1,3},{2,0},{3,1},{4,6},{5,7},{6,4},{7,5},{8,10},{9,11},{10,... | collective-permute-start | bytes 196616 | tf_op jit(solution)/shard_map/ppermute | solution.py:311
  14.4 0.2 collective-permute-start.6
  14.6 1.0 %sweep.1 = (f32[1024,128]{1,0:T(8,128)S(1)}, f32[80,128]{1,0:T(8,128)S(1)}, f32[80,128]{1,0:T(8,128)S(1)}) custom-call(s32[1]{0:T(128)} %bitcast.me, s32[1]{0:T(128)} %bitcast.1.half, f32[5,5]{1,0:T(8,128)} %jac.3, f32[5,5]{1,0:T(8,128)} %left.3, f32[256,128]{1,0:T(8,128)S(1)} %get-tuple-element.41.refs_0_, f32[256,128]{1,0:T(8,128)S(1)} %collective-permute-done.refs_1_, ...), custom_call_target="tpu_custom_call" | custom-call | tf_op jit(solution)/shard_map/sweep/pallas_call | solution.py:359
  15.6 2.8 %collective-permute-start.3 = (f32[80,128]{1,0:T(8,128)S(1)}, f32[80,128]{1,0:T(8,128)S(1)}, u32[]{:S(2)}, u32[]{:S(2)}) collective-permute-start(f32[80,128]{1,0:T(8,128)S(1)} %get-tuple-element.47.mine), channel_id=1, source_target_pairs={{0,16},{4,20},{8,24},{12,28},{16,0},{20,4},{24,8},{28,12},{1,17},{... | collective-permute-start | bytes 122888 | tf_op jit(solution)/shard_map/ppermute | solution.py:311
  18.5 2.1 %collective-permute-done.3.other = f32[80,128]{1,0:T(8,128)S(1)} collective-permute-done((f32[80,128]{1,0:T(8,128)S(1)}, f32[80,128]{1,0:T(8,128)S(1)}, u32[]{:S(2)}, u32[]{:S(2)}) %collective-permute-start.3) | collective-permute-done | bytes 40992 | tf_op jit(solution)/shard_map/ppermute | solution.py:311
  20.6 0.0 collective-permute-done.4.refs_5_
  20.6 0.0 collective-permute-done.5.refs_6_
  20.6 0.0 collective-permute-done.6.refs_7_
  20.6 1.5 %solve.1 = (f32[40,128]{1,0:T(8,128)S(1)}, f32[40,128]{1,0:T(8,128)S(1)}, f32[40,128]{1,0:T(8,128)S(1)}, f32[40,128]{1,0:T(8,128)S(1)}, f32[32,1,128]{2,1,0:T(1,128)}) custom-call(s32[1]{0:T(128)} %bitcast.me, s32[1]{0:T(128)} %bitcast.1.half, f32[5,5]{1,0:T(8,128)} %right.1, f32[1024,128]{1,0:T(8,128)S(1)} %get-tuple-element.45.lines, ...), custom_call_target="tpu_custom_call" | custom-call | tf_op jit(solution)/shard_map/solve/pallas_call | solution.py:374
  22.1 6.5 %all-to-all-start = ((f32[32,1,128]{2,1,0:T(1,128)}), f32[32,1,128]{2,1,0:T(1,128)S(1)}, u32[]{:S(2)}, u32[]{:S(2)}) async-start(f32[32,1,128]{2,1,0:T(1,128)} %get-tuple-element.53), calls=%async_computation | async-start | bytes 32768 | tf_op jit(solution)/shard_map/all_to_all | solution.py:386
  28.6 1.8 %collective-permute-start.7 = (f32[40,128]{1,0:T(8,128)S(1)}, f32[40,128]{1,0:T(8,128)S(1)}, u32[]{:S(2)}, u32[]{:S(2)}) collective-permute-start(f32[40,128]{1,0:T(8,128)S(1)} %get-tuple-element.55), channel_id=1, source_target_pairs={{0,4},{4,0},{8,12},{12,8},{16,20},{20,16},{24,28},{28,24},{1,5},{5... | collective-permute-start | bytes 61448 | tf_op jit(solution)/shard_map/ppermute | solution.py:311
  30.5 1.5 %collective-permute-start.8 = (f32[40,128]{1,0:T(8,128)S(1)}, f32[40,128]{1,0:T(8,128)S(1)}, u32[]{:S(2)}, u32[]{:S(2)}) collective-permute-start(f32[40,128]{1,0:T(8,128)S(1)} %get-tuple-element.56), channel_id=1, source_target_pairs={{0,8},{4,12},{8,0},{12,4},{16,24},{20,28},{24,16},{28,20},{1,9},{5... | collective-permute-start | bytes 61448 | tf_op jit(solution)/shard_map/ppermute | solution.py:311
  31.9 0.3 collective-permute-start.9
  32.2 0.3 collective-permute-done.7.refs_1_
  32.5 1.9 %collective-permute-done.8.refs_2_ = f32[40,128]{1,0:T(8,128)S(1)} collective-permute-done((f32[40,128]{1,0:T(8,128)S(1)}, f32[40,128]{1,0:T(8,128)S(1)}, u32[]{:S(2)}, u32[]{:S(2)}) %collective-permute-start.8) | collective-permute-done | bytes 20512 | tf_op jit(solution)/shard_map/ppermute | solution.py:311
  34.4 2.2 %collective-permute-done.9.refs_3_ = f32[40,128]{1,0:T(8,128)S(1)} collective-permute-done((f32[40,128]{1,0:T(8,128)S(1)}, f32[40,128]{1,0:T(8,128)S(1)}, u32[]{:S(2)}, u32[]{:S(2)}) %collective-permute-start.9) | collective-permute-done | bytes 20512 | tf_op jit(solution)/shard_map/ppermute | solution.py:311
  36.6 0.0 all-to-all-done.squares
  36.6 1.7 %finish.1 = (f32[5,4,1024]{2,1,0:T(4,128)}, f32[128,128]{1,0:T(8,128)}) custom-call(s32[1]{0:T(128)} %bitcast.me, f32[5,4,1024]{2,1,0:T(4,128)} %adj.5, f32[32,1,128]{2,1,0:T(1,128)S(1)} %all-to-all-done.squares, f32[40,128]{1,0:T(8,128)S(1)} %get-tuple-element.54.refs_0_, f32[40,128]{1,0:T(8,128)S(1)} %collective-permute-done.7.refs_1_, ...), custom_call_target="tpu_custom_call" | custom-call | tf_op jit(solution)/shard_map/finish/pallas_call | solution.py:390
Async XLA Ops:
  2.1 7.1 %collective-permute-start = (f32[256,128]{1,0:T(8,128)S(1)}, f32[256,128]{1,0:T(8,128)S(1)}, u32[]{:S(2)}, u32[]{:S(2)}) collective-permute-start(f32[256,128]{1,0:T(8,128)S(1)} %get-tuple-element.34), channel_id=1, source_target_pairs={{0,4},{4,0},{8,12},{12,8},{16,20},{20,16},{24,28},{28,24},{1,5},{5... | collective-permute-start | bytes 393224 | tf_op jit(solution)/shard_map/ppermute | solution.py:311
  5.2 6.4 %collective-permute-start.1 = (f32[256,128]{1,0:T(8,128)S(1)}, f32[256,128]{1,0:T(8,128)S(1)}, u32[]{:S(2)}, u32[]{:S(2)}) collective-permute-start(f32[256,128]{1,0:T(8,128)S(1)} %get-tuple-element.35), channel_id=1, source_target_pairs={{0,8},{4,12},{8,0},{12,4},{16,24},{20,28},{24,16},{28,20},{1,9},{5... | collective-permute-start | bytes 393224 | tf_op jit(solution)/shard_map/ppermute | solution.py:311
  6.7 6.0 %collective-permute-start.2 = (f32[256,128]{1,0:T(8,128)S(1)}, f32[256,128]{1,0:T(8,128)S(1)}, u32[]{:S(2)}, u32[]{:S(2)}) collective-permute-start(f32[256,128]{1,0:T(8,128)S(1)} %get-tuple-element.36), channel_id=1, source_target_pairs={{0,12},{4,8},{8,4},{12,0},{16,28},{20,24},{24,20},{28,16},{1,13},{... | collective-permute-start | bytes 393224 | tf_op jit(solution)/shard_map/ppermute | solution.py:311
  12.7 7.9 %collective-permute-start.4 = (f32[128,128]{1,0:T(8,128)S(1)}, f32[128,128]{1,0:T(8,128)S(1)}, u32[]{:S(2)}, u32[]{:S(2)}) collective-permute-start(f32[128,128]{1,0:T(8,128)S(1)} %get-tuple-element.49), channel_id=1, source_target_pairs={{0,1},{1,0},{2,3},{3,2},{4,5},{5,4},{6,7},{7,6},{8,9},{9,8},{10,11... | collective-permute-start | bytes 196616 | tf_op jit(solution)/shard_map/ppermute | solution.py:311
  12.7 7.9 %collective-permute-start.5 = (f32[128,128]{1,0:T(8,128)S(1)}, f32[128,128]{1,0:T(8,128)S(1)}, u32[]{:S(2)}, u32[]{:S(2)}) collective-permute-start(f32[128,128]{1,0:T(8,128)S(1)} %get-tuple-element.50), channel_id=1, source_target_pairs={{0,2},{1,3},{2,0},{3,1},{4,6},{5,7},{6,4},{7,5},{8,10},{9,11},{10,... | collective-permute-start | bytes 196616 | tf_op jit(solution)/shard_map/ppermute | solution.py:311
  14.4 6.2 %collective-permute-start.6 = (f32[128,128]{1,0:T(8,128)S(1)}, f32[128,128]{1,0:T(8,128)S(1)}, u32[]{:S(2)}, u32[]{:S(2)}) collective-permute-start(f32[128,128]{1,0:T(8,128)S(1)} %get-tuple-element.51), channel_id=1, source_target_pairs={{0,3},{1,2},{2,1},{3,0},{4,7},{5,6},{6,5},{7,4},{8,11},{9,10},{10,... | collective-permute-start | bytes 196616 | tf_op jit(solution)/shard_map/ppermute | solution.py:311
  15.6 5.0 %collective-permute-start.3 = (f32[80,128]{1,0:T(8,128)S(1)}, f32[80,128]{1,0:T(8,128)S(1)}, u32[]{:S(2)}, u32[]{:S(2)}) collective-permute-start(f32[80,128]{1,0:T(8,128)S(1)} %get-tuple-element.47.mine), channel_id=1, source_target_pairs={{0,16},{4,20},{8,24},{12,28},{16,0},{20,4},{24,8},{28,12},{1,17},{... | collective-permute-start | bytes 122888 | tf_op jit(solution)/shard_map/ppermute | solution.py:311
  22.1 14.5 %all-to-all-start = ((f32[32,1,128]{2,1,0:T(1,128)}), f32[32,1,128]{2,1,0:T(1,128)S(1)}, u32[]{:S(2)}, u32[]{:S(2)}) async-start(f32[32,1,128]{2,1,0:T(1,128)} %get-tuple-element.53), calls=%async_computation | async-start | bytes 32768 | tf_op jit(solution)/shard_map/all_to_all | solution.py:386
  28.6 3.9 %collective-permute-start.7 = (f32[40,128]{1,0:T(8,128)S(1)}, f32[40,128]{1,0:T(8,128)S(1)}, u32[]{:S(2)}, u32[]{:S(2)}) collective-permute-start(f32[40,128]{1,0:T(8,128)S(1)} %get-tuple-element.55), channel_id=1, source_target_pairs={{0,4},{4,0},{8,12},{12,8},{16,20},{20,16},{24,28},{28,24},{1,5},{5... | collective-permute-start | bytes 61448 | tf_op jit(solution)/shard_map/ppermute | solution.py:311
  30.5 3.9 %collective-permute-start.8 = (f32[40,128]{1,0:T(8,128)S(1)}, f32[40,128]{1,0:T(8,128)S(1)}, u32[]{:S(2)}, u32[]{:S(2)}) collective-permute-start(f32[40,128]{1,0:T(8,128)S(1)} %get-tuple-element.56), channel_id=1, source_target_pairs={{0,8},{4,12},{8,0},{12,4},{16,24},{20,28},{24,16},{28,20},{1,9},{5... | collective-permute-start | bytes 61448 | tf_op jit(solution)/shard_map/ppermute | solution.py:311
  31.9 4.7 %collective-permute-start.9 = (f32[40,128]{1,0:T(8,128)S(1)}, f32[40,128]{1,0:T(8,128)S(1)}, u32[]{:S(2)}, u32[]{:S(2)}) collective-permute-start(f32[40,128]{1,0:T(8,128)S(1)} %get-tuple-element.57), channel_id=1, source_target_pairs={{0,12},{4,8},{8,4},{12,0},{16,28},{20,24},{24,20},{28,16},{1,13},{... | collective-permute-start | bytes 61448 | tf_op jit(solution)/shard_map/ppermute | solution.py:311

commit v4 on v3

--- a/solution.py
+++ b/solution.py
@@ -328,7 +328,7 @@
     f32 = jnp.float32
 
     at = lax.axis_index("stream").astype(jnp.int32)
-    me, half = (at % group).reshape(1), (at // group).reshape(1)
+    me, half = lax.rem(at, group).reshape(1), lax.div(at, group).reshape(1)
     packed = pl.pallas_call(
         functools.partial(pack_kernel, group, width),
         out_shape=[pltpu.VMEM((rows, LANES), f32)] * group,
@@ -369,7 +369,6 @@
     )(me, half, jacobian, left_vectors, *(held(a) for a in received))
     other = swap(message, "stream", group)
     slabs = exchange(slabs, "cross")
-    other, *slabs = lax.optimization_barrier((other, *slabs))
 
     *moved, squares = pl.pallas_call(
         functools.partial(solve_kernel, group, fields, cells),

time: 38.6 us -> 36.2 us (0.938)
  waiting for transfers between devices: 10.1 us -> 7.62 us
    ppermute x10, waiting for transfers between devices: 10.1 us -> 7.05 us  [swap(): lax.ppermute(array, axis, [(i, i ^ k) for i in range(lax.axis_size(axis))])]
    ppermute x10, starting transfers between devices: 12.9 us -> 14.3 us  [swap(): lax.ppermute(array, axis, [(i, i ^ k) for i in range(lax.axis_size(axis))])]
    all_to_all x1, starting transfers between devices: 6.53 us -> 5.25 us  [shards(): lax.all_to_all(squares, ('stream', 'cross'), split_axis=0, concat_axis=0,...]
    all_to_all x1, waiting for transfers between devices: 0.01 us -> 0.57 us  [shards(): lax.all_to_all(squares, ('stream', 'cross'), split_axis=0, concat_axis=0,...]
  transfers between devices with their start and end apart: 11 -> 11, of which waited for: 6 -> 6; matrix products, arithmetic and copies ran while one was open for 0% -> 0% of each run, Pallas kernels for 9% -> 11%
where the time goes in v4:
time: 36.2 us; the launch traced here: 35.9 us
  starting transfers between devices  19.5 us (54%)
  Pallas kernels  8.11 us (22%)
  waiting for transfers between devices  7.62 us (21%)
  between operations  0.68 us (2%)
    ppermute x10, starting transfers between devices, swap(): lax.ppermute(array, axis, [(i, i ^ k) for i in range(lax.axis_size(axis))])  14.3 us
    ppermute x10, waiting for transfers between devices, swap(): lax.ppermute(array, axis, [(i, i ^ k) for i in range(lax.axis_size(axis))])  7.05 us
    all_to_all x1, starting transfers between devices, shards(): lax.all_to_all(squares, ('stream', 'cross'), split_axis=0, concat_axis=0,...  5.25 us
    pallas_call x1, Pallas kernels, shards(): pl.pallas_call(functools.partial(slab_kernel, peers), out_shape=[pltpu.VM...  2.43 us
    pallas_call x1, Pallas kernels, shards(): pl.pallas_call(functools.partial(finish_kernel, group, width, peers, cell...  1.68 us
    pallas_call x1, Pallas kernels, shards(): pl.pallas_call(functools.partial(solve_kernel, group, fields, cells), out...  1.49 us
    pallas_call x1, Pallas kernels, shards(): pl.pallas_call(functools.partial(pack_kernel, group, width), out_shape=[p...  1.47 us
    pallas_call x1, Pallas kernels, shards(): pl.pallas_call(functools.partial(sweep_kernel, group, fields, cells), out...  1.04 us
  transfers between devices with their start and end apart: 11, of which 6 were waited for; matrix products, arithmetic and copies ran while one was open for 0% of the time, Pallas kernels for 11%

profile of v4, /device:TPU:0, one launch (start us, length us, event | category | flops | bytes accessed | tf_op | source)
XLA Modules:
  0.0 35.9 jit_solution(4343683603423180569)
XLA Ops:
  0.6 1.5 %pack.1 = (f32[256,128]{1,0:T(8,128)S(1)}, f32[256,128]{1,0:T(8,128)S(1)}, f32[256,128]{1,0:T(8,128)S(1)}, f32[256,128]{1,0:T(8,128)S(1)}) custom-call(s32[1]{0:T(128)} %bitcast.me, f32[5,5]{1,0:T(8,128)} %jac.3, f32[5,5]{1,0:T(8,128)} %left.3, f32[5,4,1024]{2,1,0:T(4,128)} %adj.5, f32[5,4,1024]{2,1,0:T(4,128)} %src.1, f32[2,5,4,1024]{3,2,1,0:T(4,128)} %low.1, ...), custom_call_target="tpu_custom_call" | custom-call | tf_op jit(solution)/shard_map/pack/pallas_call | solution.py:332
  2.1 3.0 %collective-permute-start = (f32[256,128]{1,0:T(8,128)S(1)}, f32[256,128]{1,0:T(8,128)S(1)}, u32[]{:S(2)}, u32[]{:S(2)}) collective-permute-start(f32[256,128]{1,0:T(8,128)S(1)} %get-tuple-element.29), channel_id=1, source_target_pairs={{0,4},{4,0},{8,12},{12,8},{16,20},{20,16},{24,28},{28,24},{1,5},{5... | collective-permute-start | bytes 393224 | tf_op jit(solution)/shard_map/ppermute | solution.py:311
  5.1 1.6 %collective-permute-start.1 = (f32[256,128]{1,0:T(8,128)S(1)}, f32[256,128]{1,0:T(8,128)S(1)}, u32[]{:S(2)}, u32[]{:S(2)}) collective-permute-start(f32[256,128]{1,0:T(8,128)S(1)} %get-tuple-element.30), channel_id=1, source_target_pairs={{0,8},{4,12},{8,0},{12,4},{16,24},{20,28},{24,16},{28,20},{1,9},{5... | collective-permute-start | bytes 393224 | tf_op jit(solution)/shard_map/ppermute | solution.py:311
  6.7 0.0 collective-permute-start.2
  6.7 2.4 %slab.1 = (f32[128,128]{1,0:T(8,128)S(1)}, f32[128,128]{1,0:T(8,128)S(1)}, f32[128,128]{1,0:T(8,128)S(1)}, f32[128,128]{1,0:T(8,128)S(1)}) custom-call(s32[1]{0:T(128)} %bitcast.2.me, f32[5,4,1024]{2,1,0:T(4,128)} %adj.5, f32[5,4,1024]{2,1,0:T(4,128)} %grad.1, s32[4,1024]{1,0:T(4,128)} %ctrl.1), custom_call_target="tpu_custom_call" | custom-call | flops 1073741824 | bytes 4194304 | tf_op jit(solution)/shard_map/slab/pallas_call | solution.py:347
  9.2 0.0 collective-permute-done.refs_1_
  9.2 2.3 %collective-permute-done.1.refs_2_ = f32[256,128]{1,0:T(8,128)S(1)} collective-permute-done((f32[256,128]{1,0:T(8,128)S(1)}, f32[256,128]{1,0:T(8,128)S(1)}, u32[]{:S(2)}, u32[]{:S(2)}) %collective-permute-start.1) | collective-permute-done | bytes 131104 | tf_op jit(solution)/shard_map/ppermute | solution.py:311
  11.5 1.2 %collective-permute-done.2.refs_3_ = f32[256,128]{1,0:T(8,128)S(1)} collective-permute-done((f32[256,128]{1,0:T(8,128)S(1)}, f32[256,128]{1,0:T(8,128)S(1)}, u32[]{:S(2)}, u32[]{:S(2)}) %collective-permute-start.2) | collective-permute-done | bytes 131104 | tf_op jit(solution)/shard_map/ppermute | solution.py:311
  12.7 1.0 %sweep.1 = (f32[1024,128]{1,0:T(8,128)S(1)}, f32[80,128]{1,0:T(8,128)S(1)}, f32[80,128]{1,0:T(8,128)S(1)}) custom-call(s32[1]{0:T(128)} %bitcast.me, s32[1]{0:T(128)} %bitcast.1.half, f32[5,5]{1,0:T(8,128)} %jac.3, f32[5,5]{1,0:T(8,128)} %left.3, f32[256,128]{1,0:T(8,128)S(1)} %get-tuple-element.36.refs_0_, f32[256,128]{1,0:T(8,128)S(1)} %collective-permute-done.refs_1_, ...), custom_call_target="tpu_custom_call" | custom-call | tf_op jit(solution)/shard_map/sweep/pallas_call | solution.py:359
  13.8 2.8 %collective-permute-start.3 = (f32[80,128]{1,0:T(8,128)S(1)}, f32[80,128]{1,0:T(8,128)S(1)}, u32[]{:S(2)}, u32[]{:S(2)}) collective-permute-start(f32[80,128]{1,0:T(8,128)S(1)} %get-tuple-element.42.mine), channel_id=1, source_target_pairs={{0,16},{4,20},{8,24},{12,28},{16,0},{20,4},{24,8},{28,12},{1,17},{... | collective-permute-start | bytes 122888 | tf_op jit(solution)/shard_map/ppermute | solution.py:311
  16.6 0.0 collective-permute-start.7
  16.6 1.5 %collective-permute-start.8 = (f32[128,128]{1,0:T(8,128)S(1)}, f32[128,128]{1,0:T(8,128)S(1)}, u32[]{:S(2)}, u32[]{:S(2)}) collective-permute-start(f32[128,128]{1,0:T(8,128)S(1)} %get-tuple-element.50), channel_id=1, source_target_pairs={{0,2},{1,3},{2,0},{3,1},{4,6},{5,7},{6,4},{7,5},{8,10},{9,11},{10,... | collective-permute-start | bytes 196616 | tf_op jit(solution)/shard_map/ppermute | solution.py:311
  18.1 0.3 collective-permute-start.9
  18.4 0.3 collective-permute-done.3.other
  18.7 1.5 %solve.1 = (f32[40,128]{1,0:T(8,128)S(1)}, f32[40,128]{1,0:T(8,128)S(1)}, f32[40,128]{1,0:T(8,128)S(1)}, f32[40,128]{1,0:T(8,128)S(1)}, f32[32,1,128]{2,1,0:T(1,128)}) custom-call(s32[1]{0:T(128)} %bitcast.me, s32[1]{0:T(128)} %bitcast.1.half, f32[5,5]{1,0:T(8,128)} %right.1, f32[1024,128]{1,0:T(8,128)S(1)} %get-tuple-element.40.lines, ...), custom_call_target="tpu_custom_call" | custom-call | tf_op jit(solution)/shard_map/solve/pallas_call | solution.py:373
  20.2 1.7 %collective-permute-start.4 = (f32[40,128]{1,0:T(8,128)S(1)}, f32[40,128]{1,0:T(8,128)S(1)}, u32[]{:S(2)}, u32[]{:S(2)}) collective-permute-start(f32[40,128]{1,0:T(8,128)S(1)} %get-tuple-element.45), channel_id=1, source_target_pairs={{0,4},{4,0},{8,12},{12,8},{16,20},{20,16},{24,28},{28,24},{1,5},{5... | collective-permute-start | bytes 61448 | tf_op jit(solution)/shard_map/ppermute | solution.py:311
  21.9 5.2 %all-to-all-start = ((f32[32,1,128]{2,1,0:T(1,128)}), f32[32,1,128]{2,1,0:T(1,128)S(1)}, u32[]{:S(2)}, u32[]{:S(2)}) async-start(f32[32,1,128]{2,1,0:T(1,128)} %get-tuple-element.43), calls=%async_computation | async-start | bytes 32768 | tf_op jit(solution)/shard_map/all_to_all | solution.py:385
  27.1 1.8 %collective-permute-start.5 = (f32[40,128]{1,0:T(8,128)S(1)}, f32[40,128]{1,0:T(8,128)S(1)}, u32[]{:S(2)}, u32[]{:S(2)}) collective-permute-start(f32[40,128]{1,0:T(8,128)S(1)} %get-tuple-element.46), channel_id=1, source_target_pairs={{0,8},{4,12},{8,0},{12,4},{16,24},{20,28},{24,16},{28,20},{1,9},{5... | collective-permute-start | bytes 61448 | tf_op jit(solution)/shard_map/ppermute | solution.py:311
  29.0 0.0 collective-permute-done.4.refs_1_
  29.0 1.5 %collective-permute-start.6 = (f32[40,128]{1,0:T(8,128)S(1)}, f32[40,128]{1,0:T(8,128)S(1)}, u32[]{:S(2)}, u32[]{:S(2)}) collective-permute-start(f32[40,128]{1,0:T(8,128)S(1)} %get-tuple-element.47), channel_id=1, source_target_pairs={{0,12},{4,8},{8,4},{12,0},{16,28},{20,24},{24,20},{28,16},{1,13},{... | collective-permute-start | bytes 61448 | tf_op jit(solution)/shard_map/ppermute | solution.py:311
  30.4 0.6 %collective-permute-done.5.refs_2_ = f32[40,128]{1,0:T(8,128)S(1)} collective-permute-done((f32[40,128]{1,0:T(8,128)S(1)}, f32[40,128]{1,0:T(8,128)S(1)}, u32[]{:S(2)}, u32[]{:S(2)}) %collective-permute-start.5) | collective-permute-done | bytes 20512 | tf_op jit(solution)/shard_map/ppermute | solution.py:311
  31.0 2.6 %collective-permute-done.6.refs_3_ = f32[40,128]{1,0:T(8,128)S(1)} collective-permute-done((f32[40,128]{1,0:T(8,128)S(1)}, f32[40,128]{1,0:T(8,128)S(1)}, u32[]{:S(2)}, u32[]{:S(2)}) %collective-permute-start.6) | collective-permute-done | bytes 20512 | tf_op jit(solution)/shard_map/ppermute | solution.py:311
  33.6 0.0 collective-permute-done.7.refs_5_
  33.6 0.0 collective-permute-done.8.refs_6_
  33.7 0.0 collective-permute-done.9.refs_7_
  33.7 0.6 %all-to-all-done.squares = f32[32,1,128]{2,1,0:T(1,128)S(1)} async-done(((f32[32,1,128]{2,1,0:T(1,128)}), f32[32,1,128]{2,1,0:T(1,128)S(1)}, u32[]{:S(2)}, u32[]{:S(2)}) %all-to-all-start) | async-done | bytes 16416 | tf_op jit(solution)/shard_map/all_to_all | solution.py:385
  34.2 1.7 %finish.1 = (f32[5,4,1024]{2,1,0:T(4,128)}, f32[128,128]{1,0:T(8,128)}) custom-call(s32[1]{0:T(128)} %bitcast.me, f32[5,4,1024]{2,1,0:T(4,128)} %adj.5, f32[32,1,128]{2,1,0:T(1,128)S(1)} %all-to-all-done.squares, f32[40,128]{1,0:T(8,128)S(1)} %get-tuple-element.44.refs_0_, f32[40,128]{1,0:T(8,128)S(1)} %collective-permute-done.4.refs_1_, ...), custom_call_target="tpu_custom_call" | custom-call | tf_op jit(solution)/shard_map/finish/pallas_call | solution.py:389
Async XLA Ops:
  2.1 7.1 %collective-permute-start = (f32[256,128]{1,0:T(8,128)S(1)}, f32[256,128]{1,0:T(8,128)S(1)}, u32[]{:S(2)}, u32[]{:S(2)}) collective-permute-start(f32[256,128]{1,0:T(8,128)S(1)} %get-tuple-element.29), channel_id=1, source_target_pairs={{0,4},{4,0},{8,12},{12,8},{16,20},{20,16},{24,28},{28,24},{1,5},{5... | collective-permute-start | bytes 393224 | tf_op jit(solution)/shard_map/ppermute | solution.py:311
  5.1 6.4 %collective-permute-start.1 = (f32[256,128]{1,0:T(8,128)S(1)}, f32[256,128]{1,0:T(8,128)S(1)}, u32[]{:S(2)}, u32[]{:S(2)}) collective-permute-start(f32[256,128]{1,0:T(8,128)S(1)} %get-tuple-element.30), channel_id=1, source_target_pairs={{0,8},{4,12},{8,0},{12,4},{16,24},{20,28},{24,16},{28,20},{1,9},{5... | collective-permute-start | bytes 393224 | tf_op jit(solution)/shard_map/ppermute | solution.py:311
  6.7 6.0 %collective-permute-start.2 = (f32[256,128]{1,0:T(8,128)S(1)}, f32[256,128]{1,0:T(8,128)S(1)}, u32[]{:S(2)}, u32[]{:S(2)}) collective-permute-start(f32[256,128]{1,0:T(8,128)S(1)} %get-tuple-element.31), channel_id=1, source_target_pairs={{0,12},{4,8},{8,4},{12,0},{16,28},{20,24},{24,20},{28,16},{1,13},{... | collective-permute-start | bytes 393224 | tf_op jit(solution)/shard_map/ppermute | solution.py:311
  13.8 5.0 %collective-permute-start.3 = (f32[80,128]{1,0:T(8,128)S(1)}, f32[80,128]{1,0:T(8,128)S(1)}, u32[]{:S(2)}, u32[]{:S(2)}) collective-permute-start(f32[80,128]{1,0:T(8,128)S(1)} %get-tuple-element.42.mine), channel_id=1, source_target_pairs={{0,16},{4,20},{8,24},{12,28},{16,0},{20,4},{24,8},{28,12},{1,17},{... | collective-permute-start | bytes 122888 | tf_op jit(solution)/shard_map/ppermute | solution.py:311
  16.6 17.1 %collective-permute-start.7 = (f32[128,128]{1,0:T(8,128)S(1)}, f32[128,128]{1,0:T(8,128)S(1)}, u32[]{:S(2)}, u32[]{:S(2)}) collective-permute-start(f32[128,128]{1,0:T(8,128)S(1)} %get-tuple-element.49), channel_id=1, source_target_pairs={{0,1},{1,0},{2,3},{3,2},{4,5},{5,4},{6,7},{7,6},{8,9},{9,8},{10,11... | collective-permute-start | bytes 196616 | tf_op jit(solution)/shard_map/ppermute | solution.py:311
  16.6 17.1 %collective-permute-start.8 = (f32[128,128]{1,0:T(8,128)S(1)}, f32[128,128]{1,0:T(8,128)S(1)}, u32[]{:S(2)}, u32[]{:S(2)}) collective-permute-start(f32[128,128]{1,0:T(8,128)S(1)} %get-tuple-element.50), channel_id=1, source_target_pairs={{0,2},{1,3},{2,0},{3,1},{4,6},{5,7},{6,4},{7,5},{8,10},{9,11},{10,... | collective-permute-start | bytes 196616 | tf_op jit(solution)/shard_map/ppermute | solution.py:311
  18.1 15.5 %collective-permute-start.9 = (f32[128,128]{1,0:T(8,128)S(1)}, f32[128,128]{1,0:T(8,128)S(1)}, u32[]{:S(2)}, u32[]{:S(2)}) collective-permute-start(f32[128,128]{1,0:T(8,128)S(1)} %get-tuple-element.51), channel_id=1, source_target_pairs={{0,3},{1,2},{2,1},{3,0},{4,7},{5,6},{6,5},{7,4},{8,11},{9,10},{10,... | collective-permute-start | bytes 196616 | tf_op jit(solution)/shard_map/ppermute | solution.py:311
  20.2 8.8 %collective-permute-start.4 = (f32[40,128]{1,0:T(8,128)S(1)}, f32[40,128]{1,0:T(8,128)S(1)}, u32[]{:S(2)}, u32[]{:S(2)}) collective-permute-start(f32[40,128]{1,0:T(8,128)S(1)} %get-tuple-element.45), channel_id=1, source_target_pairs={{0,4},{4,0},{8,12},{12,8},{16,20},{20,16},{24,28},{28,24},{1,5},{5... | collective-permute-start | bytes 61448 | tf_op jit(solution)/shard_map/ppermute | solution.py:311
  21.9 12.4 %all-to-all-start = ((f32[32,1,128]{2,1,0:T(1,128)}), f32[32,1,128]{2,1,0:T(1,128)S(1)}, u32[]{:S(2)}, u32[]{:S(2)}) async-start(f32[32,1,128]{2,1,0:T(1,128)} %get-tuple-element.43), calls=%async_computation | async-start | bytes 32768 | tf_op jit(solution)/shard_map/all_to_all | solution.py:385
  27.1 3.9 %collective-permute-start.5 = (f32[40,128]{1,0:T(8,128)S(1)}, f32[40,128]{1,0:T(8,128)S(1)}, u32[]{:S(2)}, u32[]{:S(2)}) collective-permute-start(f32[40,128]{1,0:T(8,128)S(1)} %get-tuple-element.46), channel_id=1, source_target_pairs={{0,8},{4,12},{8,0},{12,4},{16,24},{20,28},{24,16},{28,20},{1,9},{5... | collective-permute-start | bytes 61448 | tf_op jit(solution)/shard_map/ppermute | solution.py:311
  29.0 4.7 %collective-permute-start.6 = (f32[40,128]{1,0:T(8,128)S(1)}, f32[40,128]{1,0:T(8,128)S(1)}, u32[]{:S(2)}, u32[]{:S(2)}) collective-permute-start(f32[40,128]{1,0:T(8,128)S(1)} %get-tuple-element.47), channel_id=1, source_target_pairs={{0,12},{4,8},{8,4},{12,0},{16,28},{20,24},{24,20},{28,16},{1,13},{... | collective-permute-start | bytes 61448 | tf_op jit(solution)/shard_map/ppermute | solution.py:311
